TPU v7x, 32 devices: a whole 2x2x4 slice. The times are simulated.
32 devices in a mesh: expert: 8 (over z, x), hidden: 4 (over y, core).
Axes of the slice: x: 2, y: 2, z: 4, core: 2. Of those that a mesh axis runs over, the one named last changes fastest.
Arguments:
- pixels: bfloat16 [8192, 1024], P('expert', 'hidden'), may hold values from -6 to 6
- conv_weight: float32 [9, 1024], P(None, 'hidden'), may hold values from -2.5 to 2.5
- norm_gain: float32 [1024], replicated, may hold values from 0.1 to 1.9
- router_weight: bfloat16 [1024, 8], P(None, 'expert'), may hold values from -0.375 to 0.375
- gate_weight: bfloat16 [8, 1024, 4096], P('expert', None, 'hidden'), may hold values from -0.1875 to 0.1875
- up_weight: bfloat16 [8, 1024, 4096], P('expert', None, 'hidden'), may hold values from -0.1875 to 0.1875
- down_weight: bfloat16 [8, 4096, 1024], P('expert', 'hidden'), may hold values from -0.09375 to 0.09375
- expert_ids: int32 [8192, 1], P('expert'), may hold values from 0 to 7; in each aligned block of 1024 rows (0 to 1023, 1024 to 2047, ...) at most 256 rows name the same one
- neighbours: int32 [8, 8], P('expert'), may hold values from -1 to 7, as said below
Outputs:
- block_out: bfloat16 [8192, 1024], P('expert', 'hidden')
Inputs may be any that keep to these rules, and one draw needn't show every extreme that they name: `expert_ids`: among the 1024 pixels of one tile (the rows of one device) no expert is named more than 256 times. `neighbours`: A simplified stand-in for the sphere's tile adjacency: the tiles form a grid of 2 rows by 4 columns that closes in the columns; row t lists the tiles to the north, south, west, east, northwest, northeast, southwest and southeast of tile t, and -1 stands for a place beyond the first or last grid row. Which tile stands where is arbitrary.
All inputs are finite; a program needn't handle non-finite values.
Results may differ from a plain program's by a relative error of at most 0.0055.
Values may be sent and summed in bfloat16 or wider, within the bound.
No kernel may reach another device: no remote copies, remote signals or barrier semaphores. Data moves between devices by JAX's collectives and lax.ppermute only.
A program may use at most 128 MiB of HBM per device.

v0:
```python
import jax
import jax.numpy as jnp
from jax import lax
from jax.sharding import PartitionSpec as P

TILE_SIDE = 32


epsilon = 1e-05


def shards(
    pixels,
    conv_weight,
    norm_gain,
    router_weight,
    gate_weight,
    up_weight,
    down_weight,
    expert_ids,
    neighbours,
):
    tile_side = TILE_SIDE
    tokens_dev, width_own = pixels.shape
    experts = lax.axis_size("expert")
    capacity = max(2, 2 * tokens_dev // experts)
    tile_grid = pixels.reshape(tile_side, tile_side, width_own)
    rim_cells = jnp.concatenate(
        [
            tile_grid[0],
            tile_grid[tile_side - 1],
            tile_grid[:, 0],
            tile_grid[:, tile_side - 1],
            tile_grid[0, 0][None],
            tile_grid[0, tile_side - 1][None],
            tile_grid[tile_side - 1, 0][None],
            tile_grid[tile_side - 1, tile_side - 1][None],
        ],
        axis=0,
    )
    gathered = lax.all_gather(rim_cells, "expert", axis=0, tiled=True).reshape(
        experts, 4 * tile_side + 4, width_own
    )
    tile_table = neighbours[0]
    present = (tile_table >= 0).astype(jnp.bfloat16)
    source_tile = jnp.maximum(tile_table, 0)

    def fetch_rim(direction, first_row, row_count):
        picked = lax.dynamic_index_in_dim(gathered, source_tile[direction], 0, keepdims=False)
        return (
            lax.slice_in_dim(picked, first_row, first_row + row_count, axis=0) * present[direction]
        )

    north = fetch_rim(0, tile_side, tile_side)
    south = fetch_rim(1, 0, tile_side)
    west = fetch_rim(2, 3 * tile_side, tile_side)
    east = fetch_rim(3, 2 * tile_side, tile_side)
    corner_nw = fetch_rim(4, 4 * tile_side + 3, 1)
    corner_ne = fetch_rim(5, 4 * tile_side + 2, 1)
    corner_sw = fetch_rim(6, 4 * tile_side + 1, 1)
    corner_se = fetch_rim(7, 4 * tile_side, 1)
    upper_rim = jnp.concatenate([corner_nw, north, corner_ne], axis=0)
    lower_rim = jnp.concatenate([corner_sw, south, corner_se], axis=0)
    middle = jnp.concatenate([west[:, None], tile_grid, east[:, None]], axis=1)
    padded = jnp.concatenate([upper_rim[None], middle, lower_rim[None]], axis=0).astype(jnp.float32)
    mixed = tile_grid.astype(jnp.float32)
    for row_off in range(3):
        for col_off in range(3):
            mixed = (
                mixed
                + conv_weight[3 * row_off + col_off]
                * padded[row_off : row_off + tile_side, col_off : col_off + tile_side]
            )
    conv_out = mixed.astype(jnp.bfloat16).reshape(tokens_dev, width_own)
    expert_of = expert_ids[:, 0]
    onehot = (expert_of[:, None] == jnp.arange(experts, dtype=jnp.int32)[None]).astype(jnp.bfloat16)
    lower_tri = (jnp.arange(tokens_dev)[:, None] > jnp.arange(tokens_dev)[None]).astype(
        jnp.bfloat16
    )
    earlier = jnp.dot(lower_tri, onehot, preferred_element_type=jnp.float32)
    slot_index = jnp.sum(earlier * onehot.astype(jnp.float32), axis=1).astype(jnp.int32)
    position = expert_of * capacity + slot_index
    whole = lax.all_gather(conv_out, "hidden", axis=1, tiled=True)
    wide_feats = whole.astype(jnp.float32)
    mean_sq = jnp.mean(wide_feats * wide_feats, axis=1, keepdims=True)
    normed = (wide_feats * lax.rsqrt(mean_sq + epsilon) * norm_gain).astype(jnp.bfloat16)
    buffer = jnp.zeros((experts * capacity, whole.shape[1]), jnp.bfloat16).at[position].set(normed)
    buffer = buffer.reshape(experts, capacity, whole.shape[1])
    received = lax.all_to_all(buffer, "expert", split_axis=0, concat_axis=0, tiled=True)
    row_count = received.shape[1]
    full_width = received.shape[2]
    row_block = received.reshape(experts * row_count, full_width)
    score = jnp.dot(row_block, router_weight, preferred_element_type=jnp.float32)
    weight = jax.nn.sigmoid(score)
    gate_act = jnp.dot(row_block, gate_weight[0], preferred_element_type=jnp.float32)
    up_act = jnp.dot(row_block, up_weight[0], preferred_element_type=jnp.float32)
    hidden = (jax.nn.silu(gate_act) * up_act * weight).astype(jnp.bfloat16)
    columns = down_weight[0]
    scattered = lax.psum_scatter(
        lax.dot_general(
            columns, hidden, (((0,), (1,)), ((), ())), preferred_element_type=jnp.float32
        ).astype(jnp.bfloat16),
        "hidden",
        scatter_dimension=0,
        tiled=True,
    ).astype(jnp.float32)
    outgoing = scattered.T.astype(jnp.bfloat16).reshape(experts, row_count, width_own)
    returned = lax.all_to_all(outgoing, "expert", split_axis=0, concat_axis=0, tiled=True)
    combined = returned.reshape(experts * capacity, width_own)[position]
    return (conv_out.astype(jnp.float32) + combined.astype(jnp.float32)).astype(jnp.bfloat16)


def solution(mesh):
    in_specs = (
        P("expert", "hidden"),
        P(None, "hidden"),
        P(),
        P(None, "expert"),
        P("expert", None, "hidden"),
        P("expert", None, "hidden"),
        P("expert", "hidden", None),
        P("expert", None),
        P("expert", None),
    )
    out_specs = P("expert", "hidden")
    return jax.shard_map(shards, mesh=mesh, in_specs=in_specs, out_specs=out_specs, check_vma=False)
```

profile of v0, /device:TPU:0, one launch (start us, length us, event | category | flops | bytes accessed | tf_op | source)
XLA Modules:
  0.0 315.4 jit_solution(12122587460719015992)
XLA Ops:
  6.5 0.0 copy-start
  6.5 0.0 all-gather.3.cloned.1.call-start
  6.5 0.8 compare_convert_fusion
  7.3 0.7 broadcast_maximum_fusion
  8.0 0.7 fusion.45
  18.5 0.7 fusion.42
  19.2 0.7 slice_bitcast_fusion
  20.0 1.0 fusion.41
  21.0 0.7 fusion.44
  21.7 1.0 fusion.43
  22.7 33.2 %all-gather = bf16[8,132,256]{2,1,0:T(8,128)(2,1)S(1)} all-gather(bf16[1,132,256]{2,1,0:T(8,128)(2,1)S(1)} %bitcast.99), channel_id=1, replica_groups=mesh['expert'=8,'hidden'=4] {'expert'}, dimensions={0}, use_global_device_ids=true | all-gather | bytes 608256 | tf_op jit(solution)/shard_map/all_gather | solution.py:41
  58.3 2.6 fusion.30
  63.4 2.6 fusion.33
  66.1 1.3 maximum_convert_fusion
  67.4 0.0 copy-start.4
  67.4 0.0 copy-start.2
  67.4 2.7 fusion.17
  70.1 0.0 all-gather.3.cloned.1.call-update
  70.1 0.0 reduce-scatter.2.cloned.1.call-start
  70.2 0.0 copy-done.4
  70.2 0.5 fusion.15
  70.7 23.4 %all-gather.3.cloned.1.call-done = bf16[1024,1024]{1,0:T(8,128)(2,1)} async-done(((bf16[1024,256]{1,0:T(8,128)(2,1)}), bf16[1024,1024]{1,0:T(8,128)(2,1)}) %all-gather.3.cloned.1.call-update) | async-done | bytes 2097168 | tf_op jit(solution)/shard_map/all_gather | solution.py:83
  94.1 2.1 fusion
  96.2 0.0 copy-done.2
  96.2 9.0 %scatter_custom_fusion = bf16[2048,1024]{1,0:T(8,128)(2,1)} fusion(s32[1024]{0:T(1024)S(1)} %bitcast.101, bf16[1024,1024]{1,0:T(8,128)(2,1)} %all-gather.3.cloned.1.call-done, f32[1024]{0:T(1024)S(1)} %copy-done.2, f32[1024]{0:T(1024)S(1)} %add_rsqrt_fusion, bf16[]{:T(256)} %constant.32.clone.1), kind=kCustom, calls=%fused_computation.11 | custom fusion | flops 4194304 | bytes 6299650 | tf_op jit(solution)/shard_map/scatter | solution.py:87
  105.2 0.0 copy-start.3
  105.2 99.2 %all_to_all.10 = bf16[8,256,1024]{2,1,0:T(8,128)(2,1)S(1)} all-to-all(bf16[8,256,1024]{2,1,0:T(8,128)(2,1)} %bitcast.92), channel_id=1, replica_groups=mesh['expert'=8,'hidden'=4] {'expert'}, dimensions={0} | all-to-all | bytes 8388608 | tf_op jit(solution)/shard_map/all_to_all | solution.py:89
  204.4 0.0 copy-start.1
  204.4 0.0 copy-done.3
  204.4 1.2 fusion.46
  205.6 0.7 copy-done.1
  206.3 0.0 copy-done
  206.3 6.6 %fusion.9 = f32[2048,1024]{1,0:T(8,128)} fusion(bf16[2048,1024]{1,0:T(8,128)(2,1)S(1)} %bitcast.90, bf16[1,1024,1024]{2,1,0:T(8,128)(2,1)S(1)} %copy-done), kind=kOutput, calls=%fused_computation.14 | convolution fusion | flops 4294967296 | bytes 14680064 | tf_op jit(solution)/shard_map/dot_general | solution.py:95
  213.0 14.6 %convert_bitcast_fusion = bf16[1024,2048]{0,1:T(8,128)(2,1)} fusion(f32[2048,1024]{1,0:T(8,128)} %fusion.9, bf16[2048,1024]{1,0:T(8,128)(2,1)} %bitcast.91, f32[2048]{0:T(1024)S(1)} %add_divide_fusion, bf16[1,1024,1024]{2,1,0:T(8,128)(2,1)} %param.15, bf16[1,1024,1024]{2,1,0:T(8,128)(2,1)} %param.14), kind=kOutput, calls=%fused_computation.8 | convolution fusion | flops 8606711808 | bytes 20979712 | tf_op jit(solution)/shard_map/dot_general | solution.py:100
  227.6 0.0 reduce-scatter.2.cloned.1.call-update
  227.6 42.7 %reduce-scatter.2.cloned.1.call-done = bf16[256,2048]{0,1:T(8,128)(2,1)} async-done(((bf16[1024,2048]{0,1:T(8,128)(2,1)}), bf16[256,2048]{0,1:T(8,128)(2,1)}) %reduce-scatter.2.cloned.1.call-update) | async-done | bytes 1048592 | tf_op jit(solution)/shard_map/reduce_scatter | solution.py:99
  270.3 5.5 %all-to-all-start.1 = ((bf16[8,256,256]{2,1,0:T(8,128)(2,1)}), bf16[8,256,256]{2,1,0:T(8,128)(2,1)S(1)}, u32[]{:S(2)}, u32[]{:S(2)}) async-start(bf16[8,256,256]{2,1,0:T(8,128)(2,1)} %bitcast.98), calls=%async_computation.2 | async-start | bytes 2097152 | tf_op jit(solution)/shard_map/all_to_all | solution.py:108
  275.8 25.6 %all-to-all-done.1 = bf16[8,256,256]{2,1,0:T(8,128)(2,1)S(1)} async-done(((bf16[8,256,256]{2,1,0:T(8,128)(2,1)}), bf16[8,256,256]{2,1,0:T(8,128)(2,1)S(1)}, u32[]{:S(2)}, u32[]{:S(2)}) %all-to-all-start.1) | async-done | bytes 1048608 | tf_op jit(solution)/shard_map/all_to_all | solution.py:108
  301.4 5.0 %gather_fusion = bf16[1024,256]{1,0:T(8,128)(2,1)} fusion(bf16[2048,256]{1,0:T(8,128)(2,1)S(1)} %bitcast.88, s32[1024]{0:T(1024)S(1)} %broadcast_clamp_fusion), kind=kCustom, calls=%fused_computation | custom fusion | bytes 1052672 | tf_op jit(solution)/shard_map/gather | solution.py:109
  306.4 2.1 add_convert_fusion
  (11 shorter events, 0.2 us)
Async XLA Ops:
  6.5 199.8 %copy-start = (bf16[1,1024,1024]{2,1,0:T(8,128)(2,1)S(1)}, bf16[1,1024,1024]{2,1,0:T(8,128)(2,1)}, u32[]{:S(2)}) copy-start(bf16[1,1024,1024]{2,1,0:T(8,128)(2,1)} %param.13) | copy-start | bytes 6291460
  6.5 87.6 %all-gather.3.cloned.1.call-start = ((), (), s32[]{:S(2)}) async-start(), calls=%async_computation.3 | async-start | bytes 2621440 | tf_op jit(solution)/shard_map/all_gather | solution.py:83
  67.4 2.8 copy-start.4
  67.4 28.8 %copy-start.2 = (f32[1024]{0:T(1024)S(1)}, f32[1024]{0:T(1024)}, u32[]{:S(2)}) copy-start(f32[1024]{0:T(1024)} %param.11) | copy-start | bytes 12292
  70.1 200.1 %reduce-scatter.2.cloned.1.call-start = ((), (), s32[]{:S(2)}) async-start(), calls=%async_computation.4 | async-start | bytes 5242880 | tf_op jit(solution)/shard_map/reduce_scatter | solution.py:99
  105.2 99.2 %copy-start.3 = (bf16[1024,1]{0,1:T(2,128)(2,1)S(1)}, bf16[1024,1]{0,1:T(2,128)(2,1)}, u32[]{:S(2)}) copy-start(bf16[1024,1]{0,1:T(2,128)(2,1)} %param.12) | copy-start | bytes 6148
  204.4 1.9 copy-start.1
  270.3 31.2 %all-to-all-start.1 = ((bf16[8,256,256]{2,1,0:T(8,128)(2,1)}), bf16[8,256,256]{2,1,0:T(8,128)(2,1)S(1)}, u32[]{:S(2)}, u32[]{:S(2)}) async-start(bf16[8,256,256]{2,1,0:T(8,128)(2,1)} %bitcast.98), calls=%async_computation.2 | async-start | bytes 2097152 | tf_op jit(solution)/shard_map/all_to_all | solution.py:108
Sparse Core Ops, SparseCore 0:
  70.2 23.8 all-gather.2
  227.7 42.5 reduce-scatter.1
where the time goes:
time: 316 us; the launch traced here: 315 us
  blocking collectives  132 us (42%)
  waiting for transfers between devices  91.8 us (29%)
  between operations  28.2 us (9%)
  other arithmetic  23.9 us (8%)
  matrix products  22.9 us (7%)
  local copies, waits for them, and re-layouts  10.7 us (3%)
  starting transfers between devices  5.55 us (2%)
    all_to_all x1, blocking collectives, shards(): lax.all_to_all(buffer, 'expert', split_axis=0, concat_axis=0, tiled=True)  99.2 us
    reduce_scatter x1, waiting for transfers between devices, shards(): lax.psum_scatter(lax.dot_general(columns, hidden, (((0,), (1,)), ((), ())...  42.7 us
    all_gather x1, blocking collectives, shards(): lax.all_gather(rim_cells, 'expert', axis=0, tiled=True)  33.2 us
    all_to_all x1, waiting for transfers between devices, shards(): lax.all_to_all(outgoing, 'expert', split_axis=0, concat_axis=0, tiled=True)  25.6 us
    all_gather x1, waiting for transfers between devices, shards(): whole = lax.all_gather(conv_out, 'hidden', axis=1, tiled=True)  23.4 us
    dot_general x1, matrix products, shards(): lax.dot_general(columns, hidden, (((0,), (1,)), ((), ())), preferred_elem...  14.6 us
    scatter x1, other arithmetic, shards(): jnp.zeros((experts * capacity, whole.shape[1]), jnp.bfloat16).at[position]  8.99 us
    dot_general x1, matrix products, shards(): jnp.dot(row_block, gate_weight[0], preferred_element_type=jnp.float32)  6.63 us
  transfers between devices with their start and end apart: 3, of which 3 were waited for; matrix products, arithmetic and copies ran while one was open for 0% of the time, Pallas kernels for 0%

commit v1 on v0

v1 whole, which is shorter than its diff:
```python
import functools

import jax
import jax.numpy as jnp
from jax import lax
from jax.experimental import pallas as pl
from jax.experimental.pallas import tpu as pltpu
from jax.sharding import PartitionSpec as P

SIDE = 32
EPSILON = 1e-05
CHUNKS = 2

f32 = jnp.float32
bf16 = jnp.bfloat16

VMEM = pltpu.MemorySpace.VMEM
SMEM = pltpu.MemorySpace.SMEM


def whole_vmem():
    return pl.BlockSpec(memory_space=VMEM)


def whole_smem():
    return pl.BlockSpec(memory_space=SMEM)


def params(mib):
    return pltpu.CompilerParams(vmem_limit_bytes=mib << 20)


def rim_kernel(nbr_ref, pix_ref, out_ref):
    tokens = pix_ref.shape[0]
    out_ref[...] = jnp.zeros_like(out_ref)
    last = tokens - SIDE
    line = lax.broadcasted_iota(jnp.int32, (2 * SIDE, tokens), 0)
    pixel = lax.broadcasted_iota(jnp.int32, (2 * SIDE, tokens), 1)
    wanted = jnp.where(line < SIDE, line * SIDE, (line - SIDE) * SIDE + SIDE - 1)
    pick = jnp.where(pixel == wanted, 1.0, 0.0).astype(bf16)
    columns = jnp.dot(pick, pix_ref[...], preferred_element_type=f32)

    def put(direction, piece):
        target = nbr_ref[0, direction]

        @pl.when(target >= 0)
        def _():
            out_ref[jnp.maximum(target, 0), : piece.shape[0], :] = piece

    put(0, pix_ref[:SIDE])
    put(1, pix_ref[last:])
    put(2, columns[:SIDE].astype(bf16))
    put(3, columns[SIDE:].astype(bf16))
    for direction, row in ((4, 0), (5, SIDE), (6, SIDE - 1), (7, 2 * SIDE - 1)):
        corner = columns[row : row + 1, :]
        put(direction, jnp.broadcast_to(corner, (16, corner.shape[1])).astype(bf16))


def rim_send(neighbours, pixels, experts):
    tokens, width = pixels.shape
    return pl.pallas_call(
        rim_kernel,
        out_shape=jax.ShapeDtypeStruct((experts, SIDE, width), bf16),
        in_specs=[whole_smem(), whole_vmem()],
        out_specs=whole_vmem(),
        compiler_params=params(8),
        name="rim_send",
    )(neighbours, pixels)


def shifted_rows(pix_ref, side_ref):
    tokens = pix_ref.shape[0]
    wide = pix_ref[...].astype(f32)
    side_ref[1, SIDE : SIDE + tokens, :] = wide
    side_ref[0, SIDE : SIDE + tokens, :] = pltpu.roll(wide, 1, 0)
    side_ref[2, SIDE : SIDE + tokens, :] = pltpu.roll(wide, tokens - 1, 0)


def conv_rows(side_ref, weight_ref, conv_ref):
    tokens = conv_ref.shape[0]
    step = 64

    def block(number, carry):
        start = pl.multiple_of(number * step, step)
        total = side_ref[1, pl.ds(start + SIDE, step), :]
        for a in range(3):
            for b in range(3):
                total = (
                    total
                    + weight_ref[3 * a + b : 3 * a + b + 1, :]
                    * side_ref[b, pl.ds(start + SIDE * a, step), :]
                )
        conv_ref[pl.ds(start, step), :] = total.astype(bf16)
        return carry

    lax.fori_loop(0, tokens // step, block, 0)


def send_rows(pos_row, conv, out_ref):
    rows = out_ref.shape[0]
    tokens = conv.shape[0]
    step = min(256, rows)
    for start in range(0, rows, step):
        slots = lax.broadcasted_iota(jnp.int32, (step, tokens), 0) + start
        pick = jnp.where(slots == pos_row, 1.0, 0.0).astype(bf16)
        out_ref[start : start + step, :] = jnp.dot(
            pick, conv, preferred_element_type=f32
        ).astype(bf16)


def route(ids_row, experts, capacity, chunks, split_border):
    tokens = ids_row.shape[1]
    token = lax.broadcasted_iota(jnp.int32, (1, tokens), 1)
    if split_border:
        i, j = token // SIDE, token % SIDE
        border = (i == 0) | (i == SIDE - 1) | (j == 0) | (j == SIDE - 1)
        kind = jnp.where(border, ids_row + experts, ids_row)
        kinds = 2 * experts
    else:
        kind, kinds = ids_row, experts
    onehot = jnp.where(lax.broadcasted_iota(jnp.int32, (kinds, tokens), 0) == kind, 1.0, 0.0)
    before = jnp.where(
        lax.broadcasted_iota(jnp.int32, (tokens, tokens), 0)
        < lax.broadcasted_iota(jnp.int32, (tokens, tokens), 1),
        1.0,
        0.0,
    ).astype(bf16)
    earlier = jnp.dot(onehot.astype(bf16), before, preferred_element_type=f32)
    slot = jnp.sum(onehot * earlier, axis=0, keepdims=True).astype(jnp.int32)
    if split_border:
        slot = jnp.where(border, capacity - 1 - slot, slot)
    size = capacity // chunks
    result = []
    for chunk in range(chunks):
        low = chunk * size
        inside = (slot >= low) & (slot < low + size)
        result.append(jnp.where(inside, ids_row * size + slot - low, -1))
    return result


def early_kernel(
    ids_ref, pix_ref, weight_ref, pos_ref, out_ref, side_ref, conv_ref, *, experts, capacity, chunks
):
    positions = route(ids_ref[...], experts, capacity, chunks, True)
    for chunk in range(chunks):
        pos_ref[chunk : chunk + 1, :] = positions[chunk]
    tokens, width = pix_ref.shape
    shifted_rows(pix_ref, side_ref)
    for b in range(3):
        side_ref[b, :SIDE, :] = jnp.zeros((SIDE, width), f32)
        side_ref[b, SIDE + tokens :, :] = jnp.zeros((SIDE, width), f32)
    conv_rows(side_ref, weight_ref, conv_ref)
    send_rows(positions[0], conv_ref[...], out_ref)


def early(ids_row, pixels, conv_weight, experts, capacity, chunks):
    tokens, width = pixels.shape
    rows = experts * capacity // chunks
    return pl.pallas_call(
        functools.partial(early_kernel, experts=experts, capacity=capacity, chunks=chunks),
        out_shape=(
            jax.ShapeDtypeStruct((chunks, tokens), jnp.int32),
            jax.ShapeDtypeStruct((rows, width), bf16),
        ),
        in_specs=[whole_vmem()] * 3,
        out_specs=(whole_vmem(), whole_vmem()),
        scratch_shapes=[
            pltpu.VMEM((3, tokens + 2 * SIDE, width), f32),
            pltpu.VMEM((tokens, width), bf16),
        ],
        compiler_params=params(24),
        name="early",
    )(ids_row, pixels, conv_weight)


def route_kernel(ids_ref, pos_ref, *, experts, capacity, chunks):
    positions = route(ids_ref[...], experts, capacity, chunks, False)
    for chunk in range(chunks):
        pos_ref[chunk : chunk + 1, :] = positions[chunk]


def route_only(ids_row, experts, capacity, chunks):
    return pl.pallas_call(
        functools.partial(route_kernel, experts=experts, capacity=capacity, chunks=chunks),
        out_shape=jax.ShapeDtypeStruct((chunks, ids_row.shape[1]), jnp.int32),
        in_specs=[whole_vmem()],
        out_specs=whole_vmem(),
        compiler_params=params(16),
        name="route",
    )(ids_row)


def late_kernel(nbr_ref, pos_ref, pix_ref, weight_ref, rim_ref, conv_ref, *rest, first):
    outs, side_ref = rest[:-1], rest[-1]
    tokens, width = pix_ref.shape
    shifted_rows(pix_ref, side_ref)

    def fetch(direction):
        source = nbr_ref[0, direction]
        block = rim_ref[jnp.maximum(source, 0)].astype(f32)
        return jnp.where(source >= 0, block, 0.0)

    pixel = lax.broadcasted_iota(jnp.int32, (tokens, SIDE), 0)
    line = lax.broadcasted_iota(jnp.int32, (tokens, SIDE), 1)
    column = lax.broadcasted_iota(jnp.int32, (tokens, width), 0) % SIDE
    for b, direction, edge in ((0, 2, 0), (2, 3, SIDE - 1)):
        place = jnp.where(pixel == line * SIDE + edge, 1.0, 0.0).astype(bf16)
        values = jnp.dot(place, fetch(direction).astype(bf16), preferred_element_type=f32)
        inner = side_ref[b, SIDE : SIDE + tokens, :]
        side_ref[b, SIDE : SIDE + tokens, :] = jnp.where(column == edge, values, inner)
    place = lax.broadcasted_iota(jnp.int32, (SIDE, width), 0)
    for middle, left, right, start in ((0, 4, 5, 0), (1, 6, 7, SIDE + tokens)):
        row = fetch(middle)
        side_ref[1, start : start + SIDE, :] = row
        side_ref[0, start : start + SIDE, :] = jnp.where(
            place == 0, fetch(left)[0:1, :], pltpu.roll(row, 1, 0)
        )
        side_ref[2, start : start + SIDE, :] = jnp.where(
            place == SIDE - 1, fetch(right)[0:1, :], pltpu.roll(row, SIDE - 1, 0)
        )
    conv_rows(side_ref, weight_ref, conv_ref)
    for number, out_ref in enumerate(outs):
        chunk = first + number
        send_rows(pos_ref[chunk : chunk + 1, :], conv_ref[...], out_ref)


def late(neighbours, positions, pixels, conv_weight, rim, first, rows):
    tokens, width = pixels.shape
    left = positions.shape[0] - first
    return pl.pallas_call(
        functools.partial(late_kernel, first=first),
        out_shape=(jax.ShapeDtypeStruct((tokens, width), bf16),)
        + (jax.ShapeDtypeStruct((rows, width), bf16),) * left,
        in_specs=[whole_smem()] + [whole_vmem()] * 4,
        out_specs=(whole_vmem(),) * (left + 1),
        scratch_shapes=[pltpu.VMEM((3, tokens + 2 * SIDE, width), f32)],
        compiler_params=params(24),
        name="late",
    )(neighbours, positions, pixels, conv_weight, rim)


def expert_kernel(
    own_ref,
    x0_ref,
    x1_ref,
    x2_ref,
    x3_ref,
    gain_ref,
    router_ref,
    gate_ref,
    up_ref,
    down_ref,
    keep0_ref,
    keep1_ref,
    give_ref,
    normed_ref,
):
    own = own_ref[0]
    pieces = (x0_ref, x1_ref, x2_ref, x3_ref)
    order = (own, own ^ 2, own ^ 1, own ^ 3)
    width = x0_ref.shape[1]
    square = 0.0
    for piece in pieces:
        wide = piece[...].astype(f32)
        square = square + wide * wide
    mean_sq = jnp.sum(square, axis=1, keepdims=True) * (1.0 / (width * len(pieces)))
    scale = lax.rsqrt(mean_sq + EPSILON)
    score = 0.0
    for piece, part in zip(pieces, order):
        normed = (piece[...].astype(f32) * scale * gain_ref[part]).astype(bf16)
        score = score + normed.astype(f32) * router_ref[part]
        start = pl.multiple_of(part * width, width)
        normed_ref[:, pl.ds(start, width)] = normed
    weight = jax.nn.sigmoid(jnp.sum(score, axis=1, keepdims=True))
    rows = normed_ref[...]
    gate = jnp.dot(rows, gate_ref[0], preferred_element_type=f32)
    up = jnp.dot(rows, up_ref[0], preferred_element_type=f32)
    hidden = (gate / (1.0 + jnp.exp(-gate)) * up * weight).astype(bf16)

    def columns(part):
        start = pl.multiple_of(part * width, width)
        return jnp.dot(
            hidden, down_ref[0, :, pl.ds(start, width)], preferred_element_type=f32
        ).astype(bf16)

    keep0_ref[...] = columns(order[0])
    keep1_ref[...] = columns(order[1])
    give_ref[0] = columns(order[2])
    give_ref[1] = columns(order[3])


def expert_layer(own, pieces, gain, router, gate_weight, up_weight, down_weight):
    rows, width = pieces[0].shape
    step = min(256, rows)
    x_spec = pl.BlockSpec((step, width), lambda i: (i, 0))

    def fixed(shape):
        return pl.BlockSpec(shape, lambda i: (0,) * len(shape))

    full = gate_weight.shape[1]
    return pl.pallas_call(
        expert_kernel,
        grid=(rows // step,),
        out_shape=(
            jax.ShapeDtypeStruct((rows, width), bf16),
            jax.ShapeDtypeStruct((rows, width), bf16),
            jax.ShapeDtypeStruct((2, rows, width), bf16),
        ),
        in_specs=[whole_smem()]
        + [x_spec] * 4
        + [
            fixed(gain.shape),
            fixed(router.shape),
            fixed(gate_weight.shape),
            fixed(up_weight.shape),
            fixed(down_weight.shape),
        ],
        out_specs=(x_spec, x_spec, pl.BlockSpec((2, step, width), lambda i: (0, i, 0))),
        scratch_shapes=[pltpu.VMEM((step, full), bf16)],
        compiler_params=params(40),
        cost_estimate=pl.CostEstimate(
            flops=6 * rows * full * gate_weight.shape[2],
            transcendentals=rows * gate_weight.shape[2],
            bytes_accessed=3 * 2 * full * gate_weight.shape[2] + 4 * rows * full,
        ),
        name="expert",
    )(own, *pieces, gain, router, gate_weight, up_weight, down_weight)


def combine_kernel(pos_ref, base_ref, rows_ref, out_ref, *, chunk):
    tokens, width = base_ref.shape
    rows = rows_ref.shape[0]
    step = min(256, tokens)
    for start in range(0, tokens, step):
        slots = lax.broadcasted_iota(jnp.int32, (step, rows), 1)
        pick = jnp.where(slots == pos_ref[start : start + step, chunk : chunk + 1], 1.0, 0.0)
        found = jnp.dot(pick.astype(bf16), rows_ref[...], preferred_element_type=f32)
        base = base_ref[start : start + step, :].astype(f32)
        out_ref[start : start + step, :] = (base + found).astype(bf16)


def combine(pos_col, base, rows, chunk):
    return pl.pallas_call(
        functools.partial(combine_kernel, chunk=chunk),
        out_shape=jax.ShapeDtypeStruct(base.shape, bf16),
        in_specs=[whole_vmem()] * 3,
        out_specs=whole_vmem(),
        compiler_params=params(16),
        name="combine",
    )(pos_col, base, rows)


def shards(
    pixels,
    conv_weight,
    norm_gain,
    router_weight,
    gate_weight,
    up_weight,
    down_weight,
    expert_ids,
    neighbours,
):
    tokens, width = pixels.shape
    experts = lax.axis_size("expert")
    parts = lax.axis_size("hidden")
    capacity = max(2, 2 * tokens // experts)
    chunks = CHUNKS
    size = capacity // chunks
    own = lax.axis_index("hidden").astype(jnp.int32).reshape(1)
    far = [(i, i ^ 2) for i in range(parts)]
    near = [(i, i ^ 1) for i in range(parts)]

    def exchange(rows):
        return lax.all_to_all(
            rows.reshape(experts, -1, width), "expert", split_axis=0, concat_axis=0, tiled=True
        )

    ids_row = expert_ids.reshape(1, tokens)
    rim = exchange(rim_send(neighbours, pixels, experts))
    if capacity - 4 * (SIDE - 1) >= size:
        positions, first_rows = early(ids_row, pixels, conv_weight, experts, capacity, chunks)
        conv_out, *later_rows = late(
            neighbours, positions, pixels, conv_weight, rim, 1, experts * size
        )
        sends = [first_rows] + list(later_rows)
    else:
        positions = route_only(ids_row, experts, capacity, chunks)
        conv_out, *sends = late(neighbours, positions, pixels, conv_weight, rim, 0, experts * size)
    pos_col = positions.T
    gain = norm_gain.reshape(parts, 1, width)
    router = router_weight.astype(f32).reshape(parts, 1, width)

    results = []
    for rows in sends:
        mine = exchange(rows).reshape(experts * size, width)
        across = lax.ppermute(mine, "hidden", far)
        beside = lax.ppermute(mine, "hidden", near)
        both = lax.ppermute(across, "hidden", near)
        results.append(
            expert_layer(
                own,
                (mine, across, beside, both),
                gain,
                router,
                gate_weight,
                up_weight,
                down_weight,
            )
        )
    base = conv_out
    for chunk, (keep0, keep1, give) in enumerate(results):
        got = lax.ppermute(give, "hidden", near)
        onward = (keep1.astype(f32) + got[1].astype(f32)).astype(bf16)
        arrived = lax.ppermute(onward, "hidden", far)
        total = (keep0.astype(f32) + got[0].astype(f32) + arrived.astype(f32)).astype(bf16)
        base = combine(pos_col, base, exchange(total).reshape(experts * size, width), chunk)
    return base


def solution(mesh):
    in_specs = (
        P("expert", "hidden"),
        P(None, "hidden"),
        P(),
        P(None, "expert"),
        P("expert", None, "hidden"),
        P("expert", None, "hidden"),
        P("expert", "hidden", None),
        P("expert", None),
        P("expert", None),
    )
    out_specs = P("expert", "hidden")
    return jax.shard_map(shards, mesh=mesh, in_specs=in_specs, out_specs=out_specs, check_vma=False)
```

time: 316 us -> 150 us (0.47)
  blocking collectives: 132 us -> 0 us
  Pallas kernels: 0 us -> 30.4 us
  between operations: 28.2 us -> 0.14 us
  starting transfers between devices: 5.55 us -> 33.3 us
  matrix products: 22.9 us -> 0 us
  waiting for transfers between devices: 91.8 us -> 71.7 us
  other arithmetic: 23.9 us -> 4.32 us
    all_to_all x1 -> x0, blocking collectives: 99.2 us -> none  [shards(): lax.all_to_all(buffer, 'expert', split_axis=0, concat_axis=0, tiled=True)]
    reduce_scatter x1 -> x0, waiting for transfers between devices: 42.7 us -> none  [shards(): lax.psum_scatter(lax.dot_general(columns, hidden, (((0,), (1,)), ((), ())...]
    ppermute x0 -> x10, waiting for transfers between devices: none -> 34.6 us  [the longest x2 24.4 us: shards(): arrived = lax.ppermute(onward, 'hidden', far)]
    all_gather x1 -> x0, blocking collectives: 33.2 us -> none  [shards(): lax.all_gather(rim_cells, 'expert', axis=0, tiled=True)]
    pallas_call x0 -> x7, Pallas kernels: none -> 30.4 us  [the longest x2 20.3 us: expert_layer(): pl.pallas_call(expert_kernel, grid=(rows // step,), out_shape=(jax.ShapeD...]
    all_gather x1 -> x0, waiting for transfers between devices: 23.4 us -> none  [shards(): whole = lax.all_gather(conv_out, 'hidden', axis=1, tiled=True)]
    dot_general x4 -> x0, matrix products: 22.9 us -> none  [the longest x1 14.6 us: shards(): lax.dot_general(columns, hidden, (((0,), (1,)), ((), ())), preferred_elem...]
    all_to_all x1 -> x5, starting transfers between devices: 5.51 us -> 25.7 us  [exchange(): lax.all_to_all(rows.reshape(experts, -1, width), 'expert', split_axis=0,...]
  transfers between devices with their start and end apart: 3 -> 15, of which waited for: 3 -> 7; matrix products, arithmetic and copies ran while one was open for 0% -> 3% of each run, Pallas kernels for 0% -> 18%
where the time goes in v1:
time: 150 us; the launch traced here: 149 us
  waiting for transfers between devices  71.7 us (48%)
  starting transfers between devices  33.3 us (22%)
  Pallas kernels  30.4 us (20%)
  local copies, waits for them, and re-layouts  9.15 us (6%)
  other arithmetic  4.32 us (3%)
    all_to_all x5, waiting for transfers between devices, exchange(): lax.all_to_all(rows.reshape(experts, -1, width), 'expert', split_axis=0,...  37.2 us
    all_to_all x5, starting transfers between devices, exchange(): lax.all_to_all(rows.reshape(experts, -1, width), 'expert', split_axis=0,...  25.7 us
    ppermute x2, waiting for transfers between devices, shards(): arrived = lax.ppermute(onward, 'hidden', far)  24.4 us
    pallas_call x2, Pallas kernels, expert_layer(): pl.pallas_call(expert_kernel, grid=(rows // step,), out_shape=(jax.ShapeD...  20.3 us
    ppermute x2, waiting for transfers between devices, shards(): across = lax.ppermute(mine, 'hidden', far)  10.2 us
    unnamed x32, local copies, waits for them, and re-layouts  8.93 us
    pallas_call x1, Pallas kernels, late(): pl.pallas_call(functools.partial(late_kernel, first=first), out_shape=(ja...  3.31 us
    ppermute x2, starting transfers between devices, shards(): arrived = lax.ppermute(onward, 'hidden', far)  3.29 us
  transfers between devices with their start and end apart: 15, of which 7 were waited for; matrix products, arithmetic and copies ran while one was open for 3% of the time, Pallas kernels for 18%

profile of v1, /device:TPU:0, one launch (start us, length us, event | category | flops | bytes accessed | tf_op | source)
XLA Modules:
  0.0 149.0 jit_solution(1730484063296104715)
XLA Ops:
  0.0 0.0 copy-start
  0.0 1.0 copy-done
  1.0 0.0 copy-start.6
  1.0 0.7 copy-done.6
  1.7 0.0 copy-start.2
  1.7 0.0 copy-start.4
  1.7 0.0 copy-start.14
  1.7 1.4 rim_send.1
  3.2 7.3 %all-to-all-start = ((bf16[8,32,256]{2,1,0:T(8,128)(2,1)}), bf16[8,32,256]{2,1,0:T(8,128)(2,1)S(1)}, u32[]{:S(2)}, u32[]{:S(2)}) async-start(bf16[8,32,256]{2,1,0:T(8,128)(2,1)} %rim_send.1), calls=%async_computation | async-start | bytes 262144 | tf_op jit(solution)/shard_map/all_to_all | solution.py:375
  10.4 1.0 copy-done.1
  11.5 0.7 copy-done.3
  12.2 0.7 copy-done.5
  12.9 3.0 %early.1 = (s32[2,1024]{1,0:T(2,128)S(1)}, bf16[1024,256]{1,0:T(8,128)(2,1)}) custom-call(s32[1,1024]{1,0:T(1,128)S(1)} %bitcast.44, bf16[1024,256]{1,0:T(8,128)(2,1)S(1)} %copy-done.1, f32[9,256]{1,0:T(8,128)S(1)} %copy-done.3), custom_call_target="tpu_custom_call" | custom-call | tf_op jit(solution)/shard_map/early/pallas_call | solution.py:159
  15.9 1.9 %all-to-all-done.rim_ref = bf16[8,32,256]{2,1,0:T(8,128)(2,1)S(1)} async-done(((bf16[8,32,256]{2,1,0:T(8,128)(2,1)}), bf16[8,32,256]{2,1,0:T(8,128)(2,1)S(1)}, u32[]{:S(2)}, u32[]{:S(2)}) %all-to-all-start) | async-done | bytes 131104 | tf_op jit(solution)/shard_map/all_to_all | solution.py:375
  17.8 4.1 %all-to-all-start.1 = ((bf16[8,128,256]{2,1,0:T(8,128)(2,1)}), bf16[8,128,256]{2,1,0:T(8,128)(2,1)S(1)}, u32[]{:S(2)}, u32[]{:S(2)}) async-start(bf16[8,128,256]{2,1,0:T(8,128)(2,1)} %bitcast.3), calls=%async_computation.1 | async-start | bytes 1048576 | tf_op jit(solution)/shard_map/all_to_all | solution.py:375
  21.9 0.0 copy-done.2
  21.9 0.0 copy-done.4
  21.9 0.0 copy-done.7
  21.9 3.3 %late.1 = (bf16[1024,256]{1,0:T(8,128)(2,1)S(1)}, bf16[1024,256]{1,0:T(8,128)(2,1)}) custom-call(s32[1,8]{1,0:T(1,128)S(1)} %copy-done.7, s32[2,1024]{1,0:T(2,128)S(1)} %get-tuple-element.15.pos_ref, bf16[1024,256]{1,0:T(8,128)(2,1)S(1)} %copy-done.2, f32[9,256]{1,0:T(8,128)S(1)} %copy-done.4, bf16[8,32,256]{2,1,0:T(8,128)(2,1)S(1)} %all-to-all-done.rim_ref), custom_call_target="tpu_custom_call" | custom-call | tf_op jit(solution)/shard_map/late/pallas_call | solution.py:230
  25.2 10.6 %all-to-all-done.1 = bf16[8,128,256]{2,1,0:T(8,128)(2,1)S(1)} async-done(((bf16[8,128,256]{2,1,0:T(8,128)(2,1)}), bf16[8,128,256]{2,1,0:T(8,128)(2,1)S(1)}, u32[]{:S(2)}, u32[]{:S(2)}) %all-to-all-start.1) | async-done | bytes 524320 | tf_op jit(solution)/shard_map/all_to_all | solution.py:375
  35.8 3.6 %all-to-all-start.3 = ((bf16[8,128,256]{2,1,0:T(8,128)(2,1)}), bf16[8,128,256]{2,1,0:T(8,128)(2,1)S(1)}, u32[]{:S(2)}, u32[]{:S(2)}) async-start(bf16[8,128,256]{2,1,0:T(8,128)(2,1)} %bitcast.11), calls=%async_computation.3 | async-start | bytes 1048576 | tf_op jit(solution)/shard_map/all_to_all | solution.py:375
  39.5 1.5 %collective-permute-start = (bf16[1024,256]{1,0:T(8,128)(2,1)S(1)}, bf16[1024,256]{1,0:T(8,128)(2,1)S(1)}, u32[]{:S(2)}, u32[]{:S(2)}) collective-permute-start(bf16[1024,256]{1,0:T(8,128)(2,1)S(1)} %bitcast.41), channel_id=1, source_target_pairs={{0,2},{1,3},{2,0},{3,1},{4,6},{5,7},{6,4},{7,5},{8,10},{9,11},{10,... | collective-permute-start | bytes 1572872 | tf_op jit(solution)/shard_map/ppermute | solution.py:397
  41.0 12.7 %all-to-all-done.3 = bf16[8,128,256]{2,1,0:T(8,128)(2,1)S(1)} async-done(((bf16[8,128,256]{2,1,0:T(8,128)(2,1)}), bf16[8,128,256]{2,1,0:T(8,128)(2,1)S(1)}, u32[]{:S(2)}, u32[]{:S(2)}) %all-to-all-start.3) | async-done | bytes 524320 | tf_op jit(solution)/shard_map/all_to_all | solution.py:375
  53.7 1.5 %collective-permute-start.5 = (bf16[1024,256]{1,0:T(8,128)(2,1)S(1)}, bf16[1024,256]{1,0:T(8,128)(2,1)S(1)}, u32[]{:S(2)}, u32[]{:S(2)}) collective-permute-start(bf16[1024,256]{1,0:T(8,128)(2,1)S(1)} %bitcast.38), channel_id=1, source_target_pairs={{0,2},{1,3},{2,0},{3,1},{4,6},{5,7},{6,4},{7,5},{8,10},{9,11},{10,... | collective-permute-start | bytes 1572872 | tf_op jit(solution)/shard_map/ppermute | solution.py:397
  55.2 0.0 collective-permute-start.1
  55.2 0.0 collective-permute-done.x1_ref
  55.2 0.5 collective-permute-start.2
  55.8 0.0 copy-done.15
  55.8 0.1 collective-permute-start.6
  55.8 10.2 %collective-permute-done.5.x1_ref = bf16[1024,256]{1,0:T(8,128)(2,1)S(1)} collective-permute-done((bf16[1024,256]{1,0:T(8,128)(2,1)S(1)}, bf16[1024,256]{1,0:T(8,128)(2,1)S(1)}, u32[]{:S(2)}, u32[]{:S(2)}) %collective-permute-start.5) | collective-permute-done | bytes 524320 | tf_op jit(solution)/shard_map/ppermute | solution.py:397
  66.0 0.0 collective-permute-start.7
  66.0 0.0 collective-permute-done.1.x2_ref
  66.0 0.0 collective-permute-done.2.x3_ref
  66.0 0.0 copy-done.14
  66.0 0.0 copy-start.8
  66.0 1.6 %copy-done.8 = bf16[1,1024,1024]{2,1,0:T(8,128)(2,1)S(1)} copy-done((bf16[1,1024,1024]{2,1,0:T(8,128)(2,1)S(1)}, bf16[1,1024,1024]{2,1,0:T(8,128)(2,1)}, u32[]{:S(2)}) %copy-start.8) | copy-done | bytes 2097176
  67.6 1.6 %copy-done.10 = bf16[1,1024,1024]{2,1,0:T(8,128)(2,1)S(1)} copy-done((bf16[1,1024,1024]{2,1,0:T(8,128)(2,1)S(1)}, bf16[1,1024,1024]{2,1,0:T(8,128)(2,1)}, u32[]{:S(2)}) %copy-start.10) | copy-done | bytes 2097176
  69.2 1.6 %copy-done.12 = bf16[1,1024,1024]{2,1,0:T(8,128)(2,1)S(1)} copy-done((bf16[1,1024,1024]{2,1,0:T(8,128)(2,1)S(1)}, bf16[1,1024,1024]{2,1,0:T(8,128)(2,1)}, u32[]{:S(2)}) %copy-start.12) | copy-done | bytes 2097176
  70.8 10.3 %expert.2 = (bf16[1024,256]{1,0:T(8,128)(2,1)S(1)}, bf16[1024,256]{1,0:T(8,128)(2,1)S(1)}, bf16[2,1024,256]{2,1,0:T(8,128)(2,1)S(1)}) custom-call(s32[1]{0:T(128)} %bitcast.2.own_ref, bf16[1024,256]{1,0:T(8,128)(2,1)S(1)} %bitcast.43, bf16[1024,256]{1,0:T(8,128)(2,1)S(1)} %collective-permute-done.x1_ref, bf16[1024,256]{1,0:T(8,128)(2,1)} %collective-permute-done.1.x2_ref, ...), custom_call_target="tpu_custom_call" | custom-call | flops 6442450944 | bytes 10485760 | tf_op jit(solution)/shard_map/expert/pallas_call | solution.py:301
  81.2 0.6 collective-permute-start.3
  81.8 0.0 collective-permute-done.6.x2_ref
  81.8 0.0 collective-permute-done.7.x3_ref
  81.8 0.0 copy-done.9
  81.8 0.0 copy-done.11
  81.8 0.0 copy-done.13
  81.8 10.0 %expert.3 = (bf16[1024,256]{1,0:T(8,128)(2,1)S(1)}, bf16[1024,256]{1,0:T(8,128)(2,1)S(1)}, bf16[2,1024,256]{2,1,0:T(8,128)(2,1)}) custom-call(s32[1]{0:T(128)} %bitcast.2.own_ref, bf16[1024,256]{1,0:T(8,128)(2,1)S(1)} %bitcast.40, bf16[1024,256]{1,0:T(8,128)(2,1)S(1)} %collective-permute-done.5.x1_ref, bf16[1024,256]{1,0:T(8,128)(2,1)S(1)} %collective-permute-done.6.x2_ref, ...), custom_call_target="tpu_custom_call" | custom-call | flops 6442450944 | bytes 10485760 | tf_op jit(solution)/shard_map/expert/pallas_call | solution.py:301
  91.8 0.0 collective-permute-start.8
  91.8 0.0 collective-permute-done.3
  91.8 0.1 fusion.3
  92.0 1.6 %collective-permute-start.4 = (bf16[1024,256]{1,0:T(8,128)(2,1)S(1)}, bf16[1024,256]{1,0:T(8,128)(2,1)S(1)}, u32[]{:S(2)}, u32[]{:S(2)}) collective-permute-start(bf16[1024,256]{1,0:T(8,128)(2,1)S(1)} %fusion.3), channel_id=1, source_target_pairs={{0,2},{1,3},{2,0},{3,1},{4,6},{5,7},{6,4},{7,5},{8,10},{9,11},{10,... | collective-permute-start | bytes 1572872 | tf_op jit(solution)/shard_map/ppermute | solution.py:415
  93.6 12.8 %collective-permute-done.4 = bf16[1024,256]{1,0:T(8,128)(2,1)S(1)} collective-permute-done((bf16[1024,256]{1,0:T(8,128)(2,1)S(1)}, bf16[1024,256]{1,0:T(8,128)(2,1)S(1)}, u32[]{:S(2)}, u32[]{:S(2)}) %collective-permute-start.4) | collective-permute-done | bytes 524320 | tf_op jit(solution)/shard_map/ppermute | solution.py:415
  106.4 1.0 fusion.5
  107.4 5.0 %all-to-all-start.2 = ((bf16[8,128,256]{2,1,0:T(8,128)(2,1)}), bf16[8,128,256]{2,1,0:T(8,128)(2,1)S(1)}, u32[]{:S(2)}, u32[]{:S(2)}) async-start(bf16[8,128,256]{2,1,0:T(8,128)(2,1)} %bitcast.9), calls=%async_computation.2 | async-start | bytes 1048576 | tf_op jit(solution)/shard_map/all_to_all | solution.py:375
  112.4 0.0 collective-permute-done.8
  112.4 1.2 fusion
  113.5 1.6 %collective-permute-start.9 = (bf16[1024,256]{1,0:T(8,128)(2,1)S(1)}, bf16[1024,256]{1,0:T(8,128)(2,1)S(1)}, u32[]{:S(2)}, u32[]{:S(2)}) collective-permute-start(bf16[1024,256]{1,0:T(8,128)(2,1)S(1)} %fusion), channel_id=1, source_target_pairs={{0,2},{1,3},{2,0},{3,1},{4,6},{5,7},{6,4},{7,5},{8,10},{9,11},{10,... | collective-permute-start | bytes 1572872 | tf_op jit(solution)/shard_map/ppermute | solution.py:415
  115.2 11.6 %collective-permute-done.9 = bf16[1024,256]{1,0:T(8,128)(2,1)S(1)} collective-permute-done((bf16[1024,256]{1,0:T(8,128)(2,1)S(1)}, bf16[1024,256]{1,0:T(8,128)(2,1)S(1)}, u32[]{:S(2)}, u32[]{:S(2)}) %collective-permute-start.9) | collective-permute-done | bytes 524320 | tf_op jit(solution)/shard_map/ppermute | solution.py:415
  126.8 2.0 %fusion.2 = bf16[1024,256]{1,0:T(8,128)(2,1)} fusion(bf16[1024,256]{1,0:T(8,128)(2,1)S(1)} %collective-permute-done.9, bf16[1024,256]{1,0:T(8,128)(2,1)S(1)} %get-tuple-element.22, bf16[2,1024,256]{2,1,0:T(8,128)(2,1)} %collective-permute-done.8), kind=kLoop, calls=%fused_computation.4 | loop fusion | flops 1572864 | bytes 2097152 | tf_op jit(solution)/shard_map/convert_element_type | solution.py:416
  128.8 0.0 all-to-all-done.2
  128.8 5.7 %all-to-all-start.4 = ((bf16[8,128,256]{2,1,0:T(8,128)(2,1)}), bf16[8,128,256]{2,1,0:T(8,128)(2,1)S(1)}, u32[]{:S(2)}, u32[]{:S(2)}) async-start(bf16[8,128,256]{2,1,0:T(8,128)(2,1)} %bitcast.16), calls=%async_computation.4 | async-start | bytes 1048576 | tf_op jit(solution)/shard_map/all_to_all | solution.py:375
  134.6 0.2 copy.10
  134.8 0.8 combine.2.base_ref
  135.6 11.9 %all-to-all-done.4 = bf16[8,128,256]{2,1,0:T(8,128)(2,1)S(1)} async-done(((bf16[8,128,256]{2,1,0:T(8,128)(2,1)}), bf16[8,128,256]{2,1,0:T(8,128)(2,1)S(1)}, u32[]{:S(2)}, u32[]{:S(2)}) %all-to-all-start.4) | async-done | bytes 524320 | tf_op jit(solution)/shard_map/all_to_all | solution.py:375
  147.4 1.6 %combine.3 = bf16[1024,256]{1,0:T(8,128)(2,1)} custom-call(s32[1024,2]{1,0:T(8,128)S(1)} %bitcast.35, bf16[1024,256]{1,0:T(8,128)(2,1)S(1)} %combine.2.base_ref, bf16[1024,256]{1,0:T(8,128)(2,1)S(1)} %bitcast.37), custom_call_target="tpu_custom_call" | custom-call | tf_op jit(solution)/shard_map/combine/pallas_call | solution.py:343
  (11 shorter events, 0.0 us)
Async XLA Ops:
  0.0 1.0 copy-start
  1.0 0.7 copy-start.6
  1.7 20.2 %copy-start.2 = (bf16[1024,256]{1,0:T(8,128)(2,1)S(1)}, bf16[1024,256]{1,0:T(8,128)(2,1)}, u32[]{:S(2)}) copy-start(bf16[1024,256]{1,0:T(8,128)(2,1)} %pix_ref.5) | copy-start | bytes 1572868
  1.7 20.2 %copy-start.4 = (f32[9,256]{1,0:T(8,128)S(1)}, f32[9,256]{1,0:T(8,128)}, u32[]{:S(2)}) copy-start(f32[9,256]{1,0:T(8,128)} %weight_ref.3) | copy-start | bytes 27652
  1.7 20.2 %copy-start.7 = (s32[1,8]{1,0:T(1,128)S(1)}, s32[1,8]{1,0:T(1,128)}, u32[]{:S(2)}) copy-start(s32[1,8]{1,0:T(1,128)} %nbr_ref.3) | copy-start | bytes 100
  1.7 54.1 %copy-start.15 = (bf16[1024,1]{0,1:T(2,128)(2,1)S(1)}, bf16[1024,1]{0,1:T(2,128)(2,1)}, u32[]{:S(2)}) copy-start(bf16[1024,1]{0,1:T(2,128)(2,1)} %param.12) | copy-start | bytes 6148
  1.7 64.3 %copy-start.14 = (f32[1024]{0:T(1024)S(1)}, f32[1024]{0:T(1024)}, u32[]{:S(2)}) copy-start(f32[1024]{0:T(1024)} %param.11) | copy-start | bytes 12292
  3.2 14.6 %all-to-all-start = ((bf16[8,32,256]{2,1,0:T(8,128)(2,1)}), bf16[8,32,256]{2,1,0:T(8,128)(2,1)S(1)}, u32[]{:S(2)}, u32[]{:S(2)}) async-start(bf16[8,32,256]{2,1,0:T(8,128)(2,1)} %rim_send.1), calls=%async_computation | async-start | bytes 262144 | tf_op jit(solution)/shard_map/all_to_all | solution.py:375
  10.4 1.0 copy-start.1
  11.5 0.7 copy-start.3
  12.2 0.7 copy-start.5
  17.8 18.0 %all-to-all-start.1 = ((bf16[8,128,256]{2,1,0:T(8,128)(2,1)}), bf16[8,128,256]{2,1,0:T(8,128)(2,1)S(1)}, u32[]{:S(2)}, u32[]{:S(2)}) async-start(bf16[8,128,256]{2,1,0:T(8,128)(2,1)} %bitcast.3), calls=%async_computation.1 | async-start | bytes 1048576 | tf_op jit(solution)/shard_map/all_to_all | solution.py:375
  35.8 17.9 %all-to-all-start.3 = ((bf16[8,128,256]{2,1,0:T(8,128)(2,1)}), bf16[8,128,256]{2,1,0:T(8,128)(2,1)S(1)}, u32[]{:S(2)}, u32[]{:S(2)}) async-start(bf16[8,128,256]{2,1,0:T(8,128)(2,1)} %bitcast.11), calls=%async_computation.3 | async-start | bytes 1048576 | tf_op jit(solution)/shard_map/all_to_all | solution.py:375
  39.5 15.8 %collective-permute-start = (bf16[1024,256]{1,0:T(8,128)(2,1)S(1)}, bf16[1024,256]{1,0:T(8,128)(2,1)S(1)}, u32[]{:S(2)}, u32[]{:S(2)}) collective-permute-start(bf16[1024,256]{1,0:T(8,128)(2,1)S(1)} %bitcast.41), channel_id=1, source_target_pairs={{0,2},{1,3},{2,0},{3,1},{4,6},{5,7},{6,4},{7,5},{8,10},{9,11},{10,... | collective-permute-start | bytes 1572872 | tf_op jit(solution)/shard_map/ppermute | solution.py:397
  53.7 12.3 %collective-permute-start.5 = (bf16[1024,256]{1,0:T(8,128)(2,1)S(1)}, bf16[1024,256]{1,0:T(8,128)(2,1)S(1)}, u32[]{:S(2)}, u32[]{:S(2)}) collective-permute-start(bf16[1024,256]{1,0:T(8,128)(2,1)S(1)} %bitcast.38), channel_id=1, source_target_pairs={{0,2},{1,3},{2,0},{3,1},{4,6},{5,7},{6,4},{7,5},{8,10},{9,11},{10,... | collective-permute-start | bytes 1572872 | tf_op jit(solution)/shard_map/ppermute | solution.py:397
  55.2 10.8 %collective-permute-start.1 = (bf16[1024,256]{1,0:T(8,128)(2,1)S(1)}, bf16[1024,256]{1,0:T(8,128)(2,1)}, u32[]{:S(2)}, u32[]{:S(2)}) collective-permute-start(bf16[1024,256]{1,0:T(8,128)(2,1)S(1)} %bitcast.42), channel_id=1, source_target_pairs={{0,1},{1,0},{2,3},{3,2},{4,5},{5,4},{6,7},{7,6},{8,9},{9,8},{10,11... | collective-permute-start | bytes 1572872 | tf_op jit(solution)/shard_map/ppermute | solution.py:398
  55.2 10.8 %collective-permute-start.2 = (bf16[1024,256]{1,0:T(8,128)(2,1)S(1)}, bf16[1024,256]{1,0:T(8,128)(2,1)}, u32[]{:S(2)}, u32[]{:S(2)}) collective-permute-start(bf16[1024,256]{1,0:T(8,128)(2,1)S(1)} %collective-permute-done.x1_ref), channel_id=1, source_target_pairs={{0,1},{1,0},{2,3},{3,2},{4,5},{5,4},{6,7},{7,6},{8,9},{9,8},{10,11... | collective-permute-start | bytes 1572872 | tf_op jit(solution)/shard_map/ppermute | solution.py:399
  55.8 26.0 %collective-permute-start.6 = (bf16[1024,256]{1,0:T(8,128)(2,1)S(1)}, bf16[1024,256]{1,0:T(8,128)(2,1)S(1)}, u32[]{:S(2)}, u32[]{:S(2)}) collective-permute-start(bf16[1024,256]{1,0:T(8,128)(2,1)S(1)} %bitcast.39), channel_id=1, source_target_pairs={{0,1},{1,0},{2,3},{3,2},{4,5},{5,4},{6,7},{7,6},{8,9},{9,8},{10,11... | collective-permute-start | bytes 1572872 | tf_op jit(solution)/shard_map/ppermute | solution.py:398
  66.0 15.8 %collective-permute-start.7 = (bf16[1024,256]{1,0:T(8,128)(2,1)S(1)}, bf16[1024,256]{1,0:T(8,128)(2,1)S(1)}, u32[]{:S(2)}, u32[]{:S(2)}) collective-permute-start(bf16[1024,256]{1,0:T(8,128)(2,1)S(1)} %collective-permute-done.5.x1_ref), channel_id=1, source_target_pairs={{0,1},{1,0},{2,3},{3,2},{4,5},{5,4},{6,7},{7,6},{8,9},{9,8},{10,11... | collective-permute-start | bytes 1572872 | tf_op jit(solution)/shard_map/ppermute | solution.py:399
  66.0 1.6 %copy-start.8 = (bf16[1,1024,1024]{2,1,0:T(8,128)(2,1)S(1)}, bf16[1,1024,1024]{2,1,0:T(8,128)(2,1)}, u32[]{:S(2)}) copy-start(bf16[1,1024,1024]{2,1,0:T(8,128)(2,1)} %gate_ref.3) | copy-start | bytes 6291460
  67.6 1.6 %copy-start.10 = (bf16[1,1024,1024]{2,1,0:T(8,128)(2,1)S(1)}, bf16[1,1024,1024]{2,1,0:T(8,128)(2,1)}, u32[]{:S(2)}) copy-start(bf16[1,1024,1024]{2,1,0:T(8,128)(2,1)} %up_ref.3) | copy-start | bytes 6291460
  69.2 1.6 %copy-start.12 = (bf16[1,1024,1024]{2,1,0:T(8,128)(2,1)S(1)}, bf16[1,1024,1024]{2,1,0:T(8,128)(2,1)}, u32[]{:S(2)}) copy-start(bf16[1,1024,1024]{2,1,0:T(8,128)(2,1)} %down_ref.3) | copy-start | bytes 6291460
  70.8 11.0 %copy-start.9 = (bf16[1,1024,1024]{2,1,0:T(8,128)(2,1)S(1)}, bf16[1,1024,1024]{2,1,0:T(8,128)(2,1)}, u32[]{:S(2)}) copy-start(bf16[1,1024,1024]{2,1,0:T(8,128)(2,1)} %gate_ref.3) | copy-start | bytes 6291460
  70.8 11.0 %copy-start.11 = (bf16[1,1024,1024]{2,1,0:T(8,128)(2,1)S(1)}, bf16[1,1024,1024]{2,1,0:T(8,128)(2,1)}, u32[]{:S(2)}) copy-start(bf16[1,1024,1024]{2,1,0:T(8,128)(2,1)} %up_ref.3) | copy-start | bytes 6291460
  70.8 11.0 %copy-start.13 = (bf16[1,1024,1024]{2,1,0:T(8,128)(2,1)S(1)}, bf16[1,1024,1024]{2,1,0:T(8,128)(2,1)}, u32[]{:S(2)}) copy-start(bf16[1,1024,1024]{2,1,0:T(8,128)(2,1)} %down_ref.3) | copy-start | bytes 6291460
  81.2 10.7 %collective-permute-start.3 = (bf16[2,1024,256]{2,1,0:T(8,128)(2,1)S(1)}, bf16[2,1024,256]{2,1,0:T(8,128)(2,1)S(1)}, u32[]{:S(2)}, u32[]{:S(2)}) collective-permute-start(bf16[2,1024,256]{2,1,0:T(8,128)(2,1)S(1)} %get-tuple-element.19), channel_id=1, source_target_pairs={{0,1},{1,0},{2,3},{3,2},{4,5},{5,4},{6,7},{7,6},{8,9},{9,8},{10,11... | collective-permute-start | bytes 3145736 | tf_op jit(solution)/shard_map/ppermute | solution.py:413
  91.8 20.5 %collective-permute-start.8 = (bf16[2,1024,256]{2,1,0:T(8,128)(2,1)}, bf16[2,1024,256]{2,1,0:T(8,128)(2,1)}, u32[]{:S(2)}, u32[]{:S(2)}) collective-permute-start(bf16[2,1024,256]{2,1,0:T(8,128)(2,1)} %get-tuple-element.23), channel_id=1, source_target_pairs={{0,1},{1,0},{2,3},{3,2},{4,5},{5,4},{6,7},{7,6},{8,9},{9,8},{10,11... | collective-permute-start | bytes 3145736 | tf_op jit(solution)/shard_map/ppermute | solution.py:413
  92.0 14.4 %collective-permute-start.4 = (bf16[1024,256]{1,0:T(8,128)(2,1)S(1)}, bf16[1024,256]{1,0:T(8,128)(2,1)S(1)}, u32[]{:S(2)}, u32[]{:S(2)}) collective-permute-start(bf16[1024,256]{1,0:T(8,128)(2,1)S(1)} %fusion.3), channel_id=1, source_target_pairs={{0,2},{1,3},{2,0},{3,1},{4,6},{5,7},{6,4},{7,5},{8,10},{9,11},{10,... | collective-permute-start | bytes 1572872 | tf_op jit(solution)/shard_map/ppermute | solution.py:415
  107.4 21.5 %all-to-all-start.2 = ((bf16[8,128,256]{2,1,0:T(8,128)(2,1)}), bf16[8,128,256]{2,1,0:T(8,128)(2,1)S(1)}, u32[]{:S(2)}, u32[]{:S(2)}) async-start(bf16[8,128,256]{2,1,0:T(8,128)(2,1)} %bitcast.9), calls=%async_computation.2 | async-start | bytes 1048576 | tf_op jit(solution)/shard_map/all_to_all | solution.py:375
  113.5 13.3 %collective-permute-start.9 = (bf16[1024,256]{1,0:T(8,128)(2,1)S(1)}, bf16[1024,256]{1,0:T(8,128)(2,1)S(1)}, u32[]{:S(2)}, u32[]{:S(2)}) collective-permute-start(bf16[1024,256]{1,0:T(8,128)(2,1)S(1)} %fusion), channel_id=1, source_target_pairs={{0,2},{1,3},{2,0},{3,1},{4,6},{5,7},{6,4},{7,5},{8,10},{9,11},{10,... | collective-permute-start | bytes 1572872 | tf_op jit(solution)/shard_map/ppermute | solution.py:415
  128.8 18.6 %all-to-all-start.4 = ((bf16[8,128,256]{2,1,0:T(8,128)(2,1)}), bf16[8,128,256]{2,1,0:T(8,128)(2,1)S(1)}, u32[]{:S(2)}, u32[]{:S(2)}) async-start(bf16[8,128,256]{2,1,0:T(8,128)(2,1)} %bitcast.16), calls=%async_computation.4 | async-start | bytes 1048576 | tf_op jit(solution)/shard_map/all_to_all | solution.py:375

commit v2 on v1

v2 whole, which is shorter than its diff:
```python
import functools

import jax
import jax.numpy as jnp
from jax import lax
from jax.experimental import pallas as pl
from jax.experimental.pallas import tpu as pltpu
from jax.sharding import PartitionSpec as P


SIDE = 32
EPSILON = 1e-05
SHARES = (7, 5, 4)
SPLITS = (1, 1, 1)
EXPERT_MIB = 60
LATE_MIB = 24
STRIP = 512

f32 = jnp.float32
bf16 = jnp.bfloat16

SMEM = pltpu.MemorySpace.SMEM


def in_hbm():
    return pl.BlockSpec(memory_space=pltpu.MemorySpace.HBM)


def whole_smem():
    return pl.BlockSpec(memory_space=SMEM)


def params(mib):
    return pltpu.CompilerParams(vmem_limit_bytes=mib << 20)


def put_rim(nbr_ref, pix_ref, out_ref, base):
    tokens = pix_ref.shape[0]
    last = tokens - SIDE
    line = lax.broadcasted_iota(jnp.int32, (2 * SIDE, tokens), 0)
    pixel = lax.broadcasted_iota(jnp.int32, (2 * SIDE, tokens), 1)
    wanted = jnp.where(line < SIDE, line * SIDE, (line - SIDE) * SIDE + SIDE - 1)
    pick = jnp.where(pixel == wanted, 1.0, 0.0).astype(bf16)
    columns = jnp.dot(pick, pix_ref[...], preferred_element_type=f32)
    out_ref[:, base : base + SIDE, :] = jnp.zeros(
        (out_ref.shape[0], SIDE, out_ref.shape[2]), bf16
    )

    def put(direction, piece):
        target = nbr_ref[0, direction]

        @pl.when(target >= 0)
        def _():
            out_ref[jnp.maximum(target, 0), base : base + piece.shape[0], :] = piece

    put(0, pix_ref[:SIDE])
    put(1, pix_ref[last:])
    put(2, columns[:SIDE].astype(bf16))
    put(3, columns[SIDE:].astype(bf16))
    for direction, row in ((4, 0), (5, SIDE), (6, SIDE - 1), (7, 2 * SIDE - 1)):
        corner = columns[row : row + 1, :]
        put(direction, jnp.broadcast_to(corner, (16, corner.shape[1])).astype(bf16))


def rim_kernel(nbr_ref, pix_ref, out_ref):
    put_rim(nbr_ref, pix_ref, out_ref, 0)


def rim_send(neighbours, pixels, experts):
    return pl.pallas_call(
        rim_kernel,
        out_shape=jax.ShapeDtypeStruct((experts, SIDE, pixels.shape[1]), bf16),
        in_specs=[whole_smem(), pl.BlockSpec()],
        compiler_params=params(8),
        name="rim_send",
    )(neighbours, pixels)


def shifted_rows(pix_ref, side_ref):
    tokens = pix_ref.shape[0]
    wide = pix_ref[...].astype(f32)
    side_ref[1, SIDE : SIDE + tokens, :] = wide
    side_ref[0, SIDE : SIDE + tokens, :] = pltpu.roll(wide, 1, 0)
    side_ref[2, SIDE : SIDE + tokens, :] = pltpu.roll(wide, tokens - 1, 0)


def conv_rows(side_ref, weight_ref, conv_ref):
    tokens = conv_ref.shape[0]
    step = 64

    def block(number, carry):
        start = pl.multiple_of(number * step, step)
        total = side_ref[1, pl.ds(start + SIDE, step), :]
        for a in range(3):
            for b in range(3):
                total = (
                    total
                    + weight_ref[3 * a + b : 3 * a + b + 1, :]
                    * side_ref[b, pl.ds(start + SIDE * a, step), :]
                )
        conv_ref[pl.ds(start, step), :] = total.astype(bf16)
        return carry

    lax.fori_loop(0, tokens // step, block, 0)


def send_rows(pos_row, conv, out_ref):
    experts, size = out_ref.shape[0], out_ref.shape[1]
    tokens = conv.shape[0]
    group = max(1, min(experts, 256 // size))
    while experts % group:
        group -= 1
    for first in range(0, experts, group):
        slots = lax.broadcasted_iota(jnp.int32, (group * size, tokens), 0) + first * size
        pick = jnp.where(slots == pos_row, 1.0, 0.0).astype(bf16)
        rows = jnp.dot(pick, conv, preferred_element_type=f32).astype(bf16)
        for number in range(group):
            out_ref[first + number] = rows[number * size : (number + 1) * size]


def route(ids_row, experts, capacity, sizes, split_border):
    tokens = ids_row.shape[1]
    token = lax.broadcasted_iota(jnp.int32, (1, tokens), 1)
    if split_border:
        i, j = token // SIDE, token % SIDE
        border = (i == 0) | (i == SIDE - 1) | (j == 0) | (j == SIDE - 1)
        kind = jnp.where(border, ids_row + experts, ids_row)
        kinds = 2 * experts
    else:
        kind, kinds = ids_row, experts
    onehot = jnp.where(lax.broadcasted_iota(jnp.int32, (kinds, tokens), 0) == kind, 1.0, 0.0)
    before = jnp.where(
        lax.broadcasted_iota(jnp.int32, (tokens, tokens), 0)
        < lax.broadcasted_iota(jnp.int32, (tokens, tokens), 1),
        1.0,
        0.0,
    ).astype(bf16)
    earlier = jnp.dot(onehot.astype(bf16), before, preferred_element_type=f32)
    slot = jnp.sum(onehot * earlier, axis=0, keepdims=True).astype(jnp.int32)
    if split_border:
        slot = jnp.where(border, capacity - 1 - slot, slot)
    result = []
    low = 0
    for size in sizes:
        inside = (slot >= low) & (slot < low + size)
        result.append(jnp.where(inside, ids_row * size + slot - low, -1))
        low += size
    return result


def early_kernel(
    nbr_hbm,
    ids_hbm,
    pix_hbm,
    weight_hbm,
    pos_ref,
    out_ref,
    nbr_ref,
    ids_ref,
    pix_ref,
    weight_ref,
    sems,
    side_ref,
    conv_ref,
    *,
    experts,
    capacity,
    sizes,
):
    loads = [
        pltpu.make_async_copy(source, target, sems.at[number])
        for number, (source, target) in enumerate(
            (
                (ids_hbm, ids_ref),
                (pix_hbm, pix_ref),
                (nbr_hbm, nbr_ref),
                (weight_hbm, weight_ref),
            )
        )
    ]
    for load in loads:
        load.start()
    loads[0].wait()
    positions = route(ids_ref[...], experts, capacity, sizes, True)
    for chunk, position in enumerate(positions):
        pos_ref[chunk : chunk + 1, :] = position
    for load in loads[1:]:
        load.wait()
    put_rim(nbr_ref, pix_ref, out_ref, sizes[0])
    tokens, width = pix_ref.shape
    shifted_rows(pix_ref, side_ref)
    for b in range(3):
        side_ref[b, :SIDE, :] = jnp.zeros((SIDE, width), f32)
        side_ref[b, SIDE + tokens :, :] = jnp.zeros((SIDE, width), f32)
    conv_rows(side_ref, weight_ref, conv_ref)
    send_rows(positions[0], conv_ref[...], out_ref.at[:, : sizes[0], :])


def early(neighbours, ids_row, pixels, conv_weight, experts, capacity, sizes):
    tokens, width = pixels.shape
    return pl.pallas_call(
        functools.partial(early_kernel, experts=experts, capacity=capacity, sizes=sizes),
        out_shape=(
            jax.ShapeDtypeStruct((len(sizes), tokens), jnp.int32),
            jax.ShapeDtypeStruct((experts, sizes[0] + SIDE, width), bf16),
        ),
        in_specs=[in_hbm()] * 4,
        scratch_shapes=[
            pltpu.SMEM(neighbours.shape, jnp.int32),
            pltpu.VMEM(ids_row.shape, jnp.int32),
            pltpu.VMEM(pixels.shape, bf16),
            pltpu.VMEM(conv_weight.shape, f32),
            pltpu.SemaphoreType.DMA((4,)),
            pltpu.VMEM((3, tokens + 2 * SIDE, width), f32),
            pltpu.VMEM((tokens, width), bf16),
        ],
        compiler_params=params(64),
        name="early",
    )(neighbours, ids_row, pixels, conv_weight)


def route_kernel(ids_ref, pos_ref, *, experts, capacity, sizes):
    positions = route(ids_ref[...], experts, capacity, sizes, False)
    for chunk, position in enumerate(positions):
        pos_ref[chunk : chunk + 1, :] = position


def route_only(ids_row, experts, capacity, sizes):
    return pl.pallas_call(
        functools.partial(route_kernel, experts=experts, capacity=capacity, sizes=sizes),
        out_shape=jax.ShapeDtypeStruct((len(sizes), ids_row.shape[1]), jnp.int32),
        compiler_params=params(16),
        name="route",
    )(ids_row)


def late_kernel(
    nbr_hbm, pos_ref, pix_hbm, weight_hbm, rim_ref, conv_ref, *rest, first, base
):
    outs = rest[:-5]
    nbr_ref, pix_ref, weight_ref, sems, side_ref = rest[-5:]
    loads = [
        pltpu.make_async_copy(source, target, sems.at[number])
        for number, (source, target) in enumerate(
            ((nbr_hbm, nbr_ref), (pix_hbm, pix_ref), (weight_hbm, weight_ref))
        )
    ]
    for load in loads:
        load.start()
    for load in loads:
        load.wait()
    tokens, width = pix_ref.shape
    shifted_rows(pix_ref, side_ref)

    def fetch(direction):
        source = nbr_ref[0, direction]
        block = rim_ref[jnp.maximum(source, 0), base : base + SIDE, :].astype(f32)
        return jnp.where(source >= 0, block, 0.0)

    pixel = lax.broadcasted_iota(jnp.int32, (tokens, SIDE), 0)
    line = lax.broadcasted_iota(jnp.int32, (tokens, SIDE), 1)
    column = lax.broadcasted_iota(jnp.int32, (tokens, width), 0) % SIDE
    for b, direction, edge in ((0, 2, 0), (2, 3, SIDE - 1)):
        place = jnp.where(pixel == line * SIDE + edge, 1.0, 0.0).astype(bf16)
        values = jnp.dot(place, fetch(direction).astype(bf16), preferred_element_type=f32)
        inner = side_ref[b, SIDE : SIDE + tokens, :]
        side_ref[b, SIDE : SIDE + tokens, :] = jnp.where(column == edge, values, inner)
    place = lax.broadcasted_iota(jnp.int32, (SIDE, width), 0)
    for middle, left, right, start in ((0, 4, 5, 0), (1, 6, 7, SIDE + tokens)):
        row = fetch(middle)
        side_ref[1, start : start + SIDE, :] = row
        side_ref[0, start : start + SIDE, :] = jnp.where(
            place == 0, fetch(left)[0:1, :], pltpu.roll(row, 1, 0)
        )
        side_ref[2, start : start + SIDE, :] = jnp.where(
            place == SIDE - 1, fetch(right)[0:1, :], pltpu.roll(row, SIDE - 1, 0)
        )
    conv_rows(side_ref, weight_ref, conv_ref)
    for number, out_ref in enumerate(outs):
        chunk = first + number
        send_rows(pos_ref[chunk : chunk + 1, :], conv_ref[...], out_ref)


def late(neighbours, positions, pixels, conv_weight, rim, experts, first, sizes):
    tokens, width = pixels.shape
    outs = (jax.ShapeDtypeStruct((tokens, width), bf16),) + tuple(
        jax.ShapeDtypeStruct((experts, size, width), bf16) for size in sizes[first:]
    )
    base = sizes[0] if first else 0
    return pl.pallas_call(
        functools.partial(late_kernel, first=first, base=base),
        out_shape=outs,
        in_specs=[in_hbm(), pl.BlockSpec(), in_hbm(), in_hbm(), pl.BlockSpec()],
        scratch_shapes=[
            pltpu.SMEM(neighbours.shape, jnp.int32),
            pltpu.VMEM(pixels.shape, bf16),
            pltpu.VMEM(conv_weight.shape, f32),
            pltpu.SemaphoreType.DMA((3,)),
            pltpu.VMEM((3, tokens + 2 * SIDE, width), f32),
        ],
        compiler_params=params(LATE_MIB),
        name="late",
    )(neighbours, positions, pixels, conv_weight, rim)


def expert_kernel(
    own_ref,
    x0_hbm,
    x1_hbm,
    x2_hbm,
    x3_hbm,
    gain_ref,
    router_ref,
    gate_hbm,
    up_hbm,
    down_hbm,
    keep0_ref,
    keep1_ref,
    give_ref,
    x_ref,
    normed_ref,
    hidden_ref,
    gate_ref,
    up_ref,
    down_ref,
    x_sems,
    w_sems,
    *,
    step,
    places,
):
    own = own_ref[0]
    order = (own, own ^ 2, own ^ 1, own ^ 3)
    parts, total, width = x_ref.shape
    strips = hidden_ref.shape[1] // STRIP
    starts = range(0, total, step)

    def columns(part):
        return pl.ds(pl.multiple_of(part * width, width), width)

    x_loads = [
        [
            pltpu.make_async_copy(
                source.at[pl.ds(place * total + start, step), :],
                x_ref.at[part, pl.ds(start, step), :],
                x_sems.at[block, part],
            )
            for part, (source, place) in enumerate(zip((x0_hbm, x1_hbm, x2_hbm, x3_hbm), places))
        ]
        for block, start in enumerate(starts)
    ]
    w_loads = []
    for strip in range(strips):
        here = pl.ds(strip * STRIP, STRIP)
        for source, target in ((gate_hbm, gate_ref), (up_hbm, up_ref)):
            w_loads.append(
                pltpu.make_async_copy(
                    source.at[0, :, here], target.at[strip], w_sems.at[len(w_loads)]
                )
            )
    down_load = pltpu.make_async_copy(down_hbm.at[0], down_ref, w_sems.at[len(w_loads)])
    for load in x_loads[0] + w_loads[:2]:
        load.start()
    for loads in x_loads[1:]:
        for load in loads:
            load.start()
    for load in w_loads[2:] + [down_load]:
        load.start()

    weights = []
    for strip in range(strips):
        for block, start in enumerate(starts):
            here = slice(start, start + step)
            if strip == 0:
                for load in x_loads[block]:
                    load.wait()
                square = 0.0
                for part in range(parts):
                    wide = x_ref[part, here, :].astype(f32)
                    square = square + wide * wide
                mean_sq = jnp.sum(square, axis=1, keepdims=True) * (1.0 / (width * parts))
                scale = lax.rsqrt(mean_sq + EPSILON)
                score = 0.0
                for part, place in enumerate(order):
                    wide = x_ref[part, here, :].astype(f32)
                    normed = (wide * scale * gain_ref[place]).astype(bf16)
                    score = score + normed.astype(f32) * router_ref[place]
                    normed_ref[here, columns(place)] = normed
                weights.append(jax.nn.sigmoid(jnp.sum(score, axis=1, keepdims=True)))
            rows = normed_ref[here, :]
            if block == 0:
                w_loads[2 * strip].wait()
            gate = jnp.dot(rows, gate_ref[strip], preferred_element_type=f32)
            if block == 0:
                w_loads[2 * strip + 1].wait()
            up = jnp.dot(rows, up_ref[strip], preferred_element_type=f32)
            hidden = gate / (1.0 + jnp.exp(-gate)) * up * weights[block]
            hidden_ref[here, strip * STRIP : (strip + 1) * STRIP] = hidden.astype(bf16)
    down_load.wait()
    for start in starts:
        here = slice(start, start + step)
        rows = hidden_ref[here, :]
        for target, part in zip((keep0_ref, keep1_ref, give_ref.at[0], give_ref.at[1]), order):
            target[here, :] = jnp.dot(
                rows, down_ref[:, columns(part)], preferred_element_type=f32
            ).astype(bf16)


def expert_layer(own, pieces, places, rows, gain, router, gate_weight, up_weight, down_weight):
    width = pieces[0].shape[1]
    full, units = gate_weight.shape[1:]
    step = next(n for n in (256, 192, 128, 64, 32, 16, 8) if rows % n == 0)
    blocks = rows // step
    parts = len(pieces)
    return pl.pallas_call(
        functools.partial(expert_kernel, step=step, places=places),
        out_shape=(
            jax.ShapeDtypeStruct((rows, width), bf16),
            jax.ShapeDtypeStruct((rows, width), bf16),
            jax.ShapeDtypeStruct((2, rows, width), bf16),
        ),
        in_specs=[whole_smem()]
        + [in_hbm()] * parts
        + [pl.BlockSpec(), pl.BlockSpec()]
        + [in_hbm()] * 3,
        scratch_shapes=[
            pltpu.VMEM((parts, rows, width), bf16),
            pltpu.VMEM((rows, full), bf16),
            pltpu.VMEM((rows, units), bf16),
            pltpu.VMEM((units // STRIP, full, STRIP), bf16),
            pltpu.VMEM((units // STRIP, full, STRIP), bf16),
            pltpu.VMEM((units, full), bf16),
            pltpu.SemaphoreType.DMA((blocks, parts)),
            pltpu.SemaphoreType.DMA((2 * units // STRIP + 1,)),
        ],
        compiler_params=params(EXPERT_MIB),
        cost_estimate=pl.CostEstimate(
            flops=6 * rows * full * units,
            transcendentals=rows * units,
            bytes_accessed=3 * 2 * full * units + 4 * rows * full,
        ),
        name="expert",
    )(own, *pieces, gain, router, gate_weight, up_weight, down_weight)


def combine_kernel(pos_ref, base_ref, rows_ref, out_ref, *, chunk):
    tokens, _ = base_ref.shape
    rows = rows_ref.shape[0]
    step = min(256, tokens)
    for start in range(0, tokens, step):
        slots = lax.broadcasted_iota(jnp.int32, (step, rows), 1)
        pick = jnp.where(slots == pos_ref[start : start + step, chunk : chunk + 1], 1.0, 0.0)
        found = jnp.dot(pick.astype(bf16), rows_ref[...], preferred_element_type=f32)
        base = base_ref[start : start + step, :].astype(f32)
        out_ref[start : start + step, :] = (base + found).astype(bf16)


def combine(pos_col, base, rows, chunk):
    return pl.pallas_call(
        functools.partial(combine_kernel, chunk=chunk),
        out_shape=jax.ShapeDtypeStruct(base.shape, bf16),
        compiler_params=params(16),
        name="combine",
    )(pos_col, base, rows)


def shards(
    pixels,
    conv_weight,
    norm_gain,
    router_weight,
    gate_weight,
    up_weight,
    down_weight,
    expert_ids,
    neighbours,
):
    tokens, width = pixels.shape
    experts = lax.axis_size("expert")
    parts = lax.axis_size("hidden")
    capacity = max(2, 2 * tokens // experts)
    sizes = tuple(share * capacity // sum(SHARES) for share in SHARES)
    own = lax.axis_index("hidden").astype(jnp.int32).reshape(1)
    far = [(i, i ^ 2) for i in range(parts)]
    near = [(i, i ^ 1) for i in range(parts)]

    def exchange(rows):
        return lax.all_to_all(rows, "expert", split_axis=0, concat_axis=0, tiled=True)

    ids_row = expert_ids.reshape(1, tokens)
    arrived = []
    if capacity - 4 * (SIDE - 1) >= sizes[0]:
        positions, sent = early(
            neighbours, ids_row, pixels, conv_weight, experts, capacity, sizes
        )
        rim = exchange(sent)
        arrived.append(rim[:, : sizes[0]])
    else:
        positions = route_only(ids_row, experts, capacity, sizes)
        rim = exchange(rim_send(neighbours, pixels, experts))
    first = len(arrived)
    conv_out, *sends = late(neighbours, positions, pixels, conv_weight, rim, experts, first, sizes)
    for sent in sends:
        arrived.append(exchange(sent))
    gain = norm_gain.reshape(parts, 1, width)
    router = router_weight.astype(f32).reshape(parts, 1, width)

    ready = []
    for chunk, rows in enumerate(arrived):
        mine = rows.reshape(-1, width)
        count = mine.shape[0] // SPLITS[chunk]
        beside = lax.ppermute(mine, "hidden", near)
        whole = []
        for split in range(SPLITS[chunk]):
            across = lax.ppermute(
                mine[split * count : (split + 1) * count], "hidden", far
            )
            both = lax.ppermute(across, "hidden", near)
            keep0, keep1, give = expert_layer(
                own,
                (mine, across, beside, both),
                (split, 0, split, 0),
                count,
                gain,
                router,
                gate_weight,
                up_weight,
                down_weight,
            )
            got = lax.ppermute(give, "hidden", near)
            onward = (keep1.astype(f32) + got[1].astype(f32)).astype(bf16)
            last = lax.ppermute(onward, "hidden", far)
            whole.append(
                (keep0.astype(f32) + got[0].astype(f32) + last.astype(f32)).astype(bf16)
            )
        ready.append(jnp.concatenate(whole, axis=0) if len(whole) > 1 else whole[0])
    base = conv_out
    pos_col = positions.T
    for chunk, rows in enumerate(ready):
        back = exchange(rows.reshape(experts, sizes[chunk], width))
        base = combine(pos_col, base, back.reshape(-1, width), chunk)
    return base


def solution(mesh):
    in_specs = (
        P("expert", "hidden"),
        P(None, "hidden"),
        P(),
        P(None, "expert"),
        P("expert", None, "hidden"),
        P("expert", None, "hidden"),
        P("expert", "hidden", None),
        P("expert", None),
        P("expert", None),
    )
    out_specs = P("expert", "hidden")
    return jax.shard_map(shards, mesh=mesh, in_specs=in_specs, out_specs=out_specs, check_vma=False)
```

time: 150 us -> 170 us (1.13)
  blocking collectives: 0 us -> 52 us
  waiting for transfers between devices: 71.7 us -> 40.6 us
  Pallas kernels: 30.4 us -> 41 us
  starting transfers between devices: 33.3 us -> 23.8 us
  local copies, waits for them, and re-layouts: 9.15 us -> 4.95 us
  other arithmetic: 4.32 us -> 6.21 us
    all_to_all x0 -> x3, blocking collectives: none -> 52 us  [exchange(): lax.all_to_all(rows, 'expert', split_axis=0, concat_axis=0, tiled=True)]
    all_to_all x5 -> x3, waiting for transfers between devices: 37.2 us -> 10.8 us  [exchange(): lax.all_to_all(rows, 'expert', split_axis=0, concat_axis=0, tiled=True)]
    all_to_all x5 -> x3, starting transfers between devices: 25.7 us -> 15.3 us  [exchange(): lax.all_to_all(rows, 'expert', split_axis=0, concat_axis=0, tiled=True)]
    pallas_call x4, Pallas kernels: 25.1 us -> 34.2 us  [the longest x3 31.6 us: expert_layer(): pl.pallas_call(functools.partial(expert_kernel, step=step, places=places)...]
    ppermute x4 -> x6, waiting for transfers between devices: 34.5 us -> 29.8 us  [the longest x3 21.6 us: shards(): lax.ppermute(mine[split * count:(split + 1) * count], 'hidden', far)]
    unnamed x32, local copies, waits for them, and re-layouts: 8.93 us -> 4.7 us
    ppermute x4 -> x6, starting transfers between devices: 6.33 us -> 7.24 us  [the longest x3 3.67 us: shards(): last = lax.ppermute(onward, 'hidden', far)]
    convert_element_type x2 -> x3, other arithmetic: 3.01 us -> 3.52 us  [shards(): (keep0.astype(f32) + got[0].astype(f32) + last.astype(f32)).astype(bf16)]
  transfers between devices with their start and end apart: 15 -> 18, of which waited for: 7 -> 7; matrix products, arithmetic and copies ran while one was open for 3% -> 4% of each run, Pallas kernels for 18% -> 20%
where the time goes in v2:
time: 170 us; the launch traced here: 169 us
  blocking collectives  52 us (31%)
  Pallas kernels  41 us (24%)
  waiting for transfers between devices  40.6 us (24%)
  starting transfers between devices  23.8 us (14%)
  other arithmetic  6.21 us (4%)
  local copies, waits for them, and re-layouts  4.95 us (3%)
    all_to_all x3, blocking collectives, exchange(): lax.all_to_all(rows, 'expert', split_axis=0, concat_axis=0, tiled=True)  52 us
    pallas_call x3, Pallas kernels, expert_layer(): pl.pallas_call(functools.partial(expert_kernel, step=step, places=places)...  31.6 us
    ppermute x3, waiting for transfers between devices, shards(): lax.ppermute(mine[split * count:(split + 1) * count], 'hidden', far)  21.6 us
    all_to_all x3, starting transfers between devices, exchange(): lax.all_to_all(rows, 'expert', split_axis=0, concat_axis=0, tiled=True)  15.3 us
    all_to_all x3, waiting for transfers between devices, exchange(): lax.all_to_all(rows, 'expert', split_axis=0, concat_axis=0, tiled=True)  10.8 us
    ppermute x3, waiting for transfers between devices, shards(): last = lax.ppermute(onward, 'hidden', far)  8.2 us
    unnamed x32, local copies, waits for them, and re-layouts  4.7 us
    pallas_call x1, Pallas kernels, early(): pl.pallas_call(functools.partial(early_kernel, experts=experts, capacity=...  3.97 us
  transfers between devices with their start and end apart: 18, of which 7 were waited for; matrix products, arithmetic and copies ran while one was open for 4% of the time, Pallas kernels for 20%

profile of v2, /device:TPU:0, one launch (start us, length us, event | category | flops | bytes accessed | tf_op | source)
XLA Modules:
  0.0 168.8 jit_solution(5157503104554168915)
XLA Ops:
  0.0 4.0 %early.1 = (s32[3,1024]{1,0:T(4,128)}, bf16[8,144,256]{2,1,0:T(8,128)(2,1)}) custom-call(s32[1,8]{1,0:T(1,128)} %nbr_hbm.3, s32[1,1024]{1,0:T(1,128)} %bitcast.57, bf16[1024,256]{1,0:T(8,128)(2,1)} %pix_hbm.3, f32[9,256]{1,0:T(8,128)} %weight_hbm.3), custom_call_target="tpu_custom_call" | custom-call | tf_op jit(solution)/shard_map/early/pallas_call | solution.py:201
  4.0 0.0 copy-start.11
  4.0 23.8 %all_to_all.30.rim_ref = bf16[8,144,256]{2,1,0:T(8,128)(2,1)S(1)} all-to-all(bf16[8,144,256]{2,1,0:T(8,128)(2,1)} %get-tuple-element.20), channel_id=1, replica_groups=mesh['expert'=8,'hidden'=4] {'expert'}, dimensions={0} | all-to-all | bytes 1179648 | tf_op jit(solution)/shard_map/all_to_all | solution.py:488
  27.8 1.0 copy-done
  28.9 0.7 copy-done.1
  29.6 0.7 copy-done.2
  30.3 0.7 copy-done.4
  30.9 2.6 %late.1 = (bf16[1024,256]{1,0:T(8,128)(2,1)S(1)}, bf16[8,80,256]{2,1,0:T(8,128)(2,1)S(1)}, bf16[8,64,256]{2,1,0:T(8,128)(2,1)S(1)}) custom-call(s32[1,8]{1,0:T(1,128)S(1)} %copy-done.4, s32[3,1024]{1,0:T(4,128)S(1)} %copy-done.2, bf16[1024,256]{1,0:T(8,128)(2,1)S(1)} %copy-done, f32[9,256]{1,0:T(8,128)S(1)} %copy-done.1, ...), custom_call_target="tpu_custom_call" | custom-call | tf_op jit(solution)/shard_map/late/pallas_call | solution.py:290
  33.6 13.6 %all_to_all.31 = bf16[8,80,256]{2,1,0:T(8,128)(2,1)S(1)} all-to-all(bf16[8,80,256]{2,1,0:T(8,128)(2,1)S(1)} %get-tuple-element.25), channel_id=1, replica_groups=mesh['expert'=8,'hidden'=4] {'expert'}, dimensions={0} | all-to-all | bytes 655360 | tf_op jit(solution)/shard_map/all_to_all | solution.py:488
  47.2 1.5 collective-permute-start.5
  48.7 0.0 copy-start.6
  48.7 0.6 collective-permute-start
  49.3 0.0 collective-permute-start.6
  49.3 8.4 %collective-permute-done.5.x1_hbm = bf16[640,256]{1,0:T(8,128)(2,1)S(1)} collective-permute-done((bf16[640,256]{1,0:T(8,128)(2,1)S(1)}, bf16[640,256]{1,0:T(8,128)(2,1)S(1)}, u32[]{:S(2)}, u32[]{:S(2)}) %collective-permute-start.5) | collective-permute-done | bytes 327712 | tf_op jit(solution)/shard_map/ppermute | solution.py:515
  57.8 0.0 collective-permute-start.7
  57.8 0.5 collective-permute-start.1
  58.3 5.8 %collective-permute-done.x1_hbm = bf16[896,256]{1,0:T(8,128)(2,1)S(1)} collective-permute-done((bf16[896,256]{1,0:T(8,128)(2,1)S(1)}, bf16[896,256]{1,0:T(8,128)(2,1)S(1)}, u32[]{:S(2)}, u32[]{:S(2)}) %collective-permute-start) | collective-permute-done | bytes 458784 | tf_op jit(solution)/shard_map/ppermute | solution.py:515
  64.1 0.0 collective-permute-start.2
  64.1 0.0 copy-done.11
  64.1 0.6 convert.7.router_ref
  64.7 0.0 collective-permute-done.6.x2_hbm
  64.7 0.0 collective-permute-done.7.x3_hbm
  64.8 10.2 %expert.4 = (bf16[640,256]{1,0:T(8,128)(2,1)}, bf16[640,256]{1,0:T(8,128)(2,1)}, bf16[2,640,256]{2,1,0:T(8,128)(2,1)}) custom-call(s32[1]{0:T(128)} %bitcast.2.own_ref, bf16[640,256]{1,0:T(8,128)(2,1)} %bitcast.56, bf16[640,256]{1,0:T(8,128)(2,1)} %copy-done.15, bf16[640,256]{1,0:T(8,128)(2,1)} %collective-permute-done.6.x2_hbm, ...), custom_call_target="tpu_custom_call" | custom-call | flops 4026531840 | bytes 8912896 | tf_op jit(solution)/shard_map/expert/pallas_call | solution.py:415
  75.0 0.5 collective-permute-start.8
  75.6 0.0 collective-permute-done.1.x2_hbm
  75.6 0.0 collective-permute-done.2.x3_hbm
  75.6 0.8 copy-done.13
  76.3 0.8 copy-done.14
  77.1 13.3 %expert.3 = (bf16[896,256]{1,0:T(8,128)(2,1)}, bf16[896,256]{1,0:T(8,128)(2,1)}, bf16[2,896,256]{2,1,0:T(8,128)(2,1)}) custom-call(s32[1]{0:T(128)} %bitcast.2.own_ref, bf16[896,256]{1,0:T(8,128)(2,1)} %bitcast.53, bf16[896,256]{1,0:T(8,128)(2,1)} %copy-done.12, bf16[896,256]{1,0:T(8,128)(2,1)} %copy-done.13, bf16[896,256]{1,0:T(8,128)(2,1)} %copy-done.14, ...), custom_call_target="tpu_custom_call" | custom-call | flops 5637144576 | bytes 9961472 | tf_op jit(solution)/shard_map/expert/pallas_call | solution.py:415
  90.4 0.1 collective-permute-start.3
  90.6 14.5 %all_to_all.32 = bf16[8,64,256]{2,1,0:T(8,128)(2,1)} all-to-all(bf16[8,64,256]{2,1,0:T(8,128)(2,1)S(1)} %get-tuple-element.29), channel_id=1, replica_groups=mesh['expert'=8,'hidden'=4] {'expert'}, dimensions={0} | all-to-all | bytes 524288 | tf_op jit(solution)/shard_map/all_to_all | solution.py:488
  105.1 1.5 collective-permute-start.10
  106.6 0.0 collective-permute-done.8
  106.6 0.1 fusion.3
  106.7 0.6 collective-permute-start.9
  107.3 0.0 collective-permute-start.11
  107.3 7.3 %collective-permute-done.10.x1_hbm = bf16[512,256]{1,0:T(8,128)(2,1)} collective-permute-done((bf16[512,256]{1,0:T(8,128)(2,1)}, bf16[512,256]{1,0:T(8,128)(2,1)}, u32[]{:S(2)}, u32[]{:S(2)}) %collective-permute-start.10) | collective-permute-done | bytes 262176 | tf_op jit(solution)/shard_map/ppermute | solution.py:515
  114.6 0.0 collective-permute-start.12
  114.6 0.0 collective-permute-done.3
  114.6 1.9 %fusion = bf16[896,256]{1,0:T(8,128)(2,1)} fusion(bf16[896,256]{1,0:T(8,128)(2,1)} %get-tuple-element.24, bf16[2,896,256]{2,1,0:T(8,128)(2,1)S(1)} %collective-permute-done.3), kind=kLoop, calls=%fused_computation.1 | loop fusion | flops 917504 | bytes 1376256 | tf_op jit(solution)/shard_map/convert_element_type | solution.py:531
  116.5 1.5 collective-permute-start.4
  118.0 1.3 collective-permute-done.9
  119.3 0.8 fusion.5
  120.1 5.5 %all-to-all-start.3 = ((bf16[8,80,256]{2,1,0:T(8,128)(2,1)}), bf16[8,80,256]{2,1,0:T(8,128)(2,1)S(1)}, u32[]{:S(2)}, u32[]{:S(2)}) async-start(bf16[8,80,256]{2,1,0:T(8,128)(2,1)} %bitcast.14), calls=%async_computation.3 | async-start | bytes 655360 | tf_op jit(solution)/shard_map/all_to_all | solution.py:488
  125.7 0.0 collective-permute-done.11.x2_hbm
  125.7 0.0 collective-permute-done.12.x3_hbm
  125.7 8.1 %expert.5 = (bf16[512,256]{1,0:T(8,128)(2,1)}, bf16[512,256]{1,0:T(8,128)(2,1)}, bf16[2,512,256]{2,1,0:T(8,128)(2,1)}) custom-call(s32[1]{0:T(128)} %bitcast.2.own_ref, bf16[512,256]{1,0:T(8,128)(2,1)} %bitcast.16.x0_hbm, bf16[512,256]{1,0:T(8,128)(2,1)} %collective-permute-done.10.x1_hbm, bf16[512,256]{1,0:T(8,128)(2,1)} %collective-permute-done.11.x2_hbm, ...), custom_call_target="tpu_custom_call" | custom-call | flops 3221225472 | bytes 8388608 | tf_op jit(solution)/shard_map/expert/pallas_call | solution.py:415
  133.8 0.1 collective-permute-start.13
  133.9 0.0 collective-permute-done.4
  133.9 0.9 fusion.2
  134.8 0.0 all-to-all-done.3
  134.8 6.1 %all-to-all-start.1 = ((bf16[8,112,256]{2,1,0:T(8,128)(2,1)}), bf16[8,112,256]{2,1,0:T(8,128)(2,1)S(1)}, u32[]{:S(2)}, u32[]{:S(2)}) async-start(bf16[8,112,256]{2,1,0:T(8,128)(2,1)} %bitcast.8), calls=%async_computation.1 | async-start | bytes 917504 | tf_op jit(solution)/shard_map/all_to_all | solution.py:488
  141.0 0.0 collective-permute-done.13
  141.0 0.1 fusion.6
  141.0 1.6 collective-permute-start.14
  142.6 6.9 %collective-permute-done.14 = bf16[512,256]{1,0:T(8,128)(2,1)S(1)} collective-permute-done((bf16[512,256]{1,0:T(8,128)(2,1)S(1)}, bf16[512,256]{1,0:T(8,128)(2,1)S(1)}, u32[]{:S(2)}, u32[]{:S(2)}) %collective-permute-start.14) | collective-permute-done | bytes 262176 | tf_op jit(solution)/shard_map/ppermute | solution.py:532
  149.5 1.7 %fusion.8 = bf16[512,256]{1,0:T(8,128)(2,1)} fusion(bf16[512,256]{1,0:T(8,128)(2,1)S(1)} %collective-permute-done.14, bf16[512,256]{1,0:T(8,128)(2,1)} %get-tuple-element.30, bf16[2,512,256]{2,1,0:T(8,128)(2,1)S(1)} %collective-permute-done.13), kind=kLoop, calls=%fused_computation.14 | loop fusion | flops 786432 | bytes 1048576 | tf_op jit(solution)/shard_map/convert_element_type | solution.py:534
  151.3 3.4 %all-to-all-done.1 = bf16[8,112,256]{2,1,0:T(8,128)(2,1)S(1)} async-done(((bf16[8,112,256]{2,1,0:T(8,128)(2,1)}), bf16[8,112,256]{2,1,0:T(8,128)(2,1)S(1)}, u32[]{:S(2)}, u32[]{:S(2)}) %all-to-all-start.1) | async-done | bytes 458784 | tf_op jit(solution)/shard_map/all_to_all | solution.py:488
  154.7 3.6 %all-to-all-start.5 = ((bf16[8,64,256]{2,1,0:T(8,128)(2,1)}), bf16[8,64,256]{2,1,0:T(8,128)(2,1)S(1)}, u32[]{:S(2)}, u32[]{:S(2)}) async-start(bf16[8,64,256]{2,1,0:T(8,128)(2,1)} %bitcast.19), calls=%async_computation.5 | async-start | bytes 524288 | tf_op jit(solution)/shard_map/all_to_all | solution.py:488
  158.3 0.2 copy.10
  158.6 0.8 combine.3.base_ref
  159.3 0.7 combine.4.base_ref
  160.0 7.4 %all-to-all-done.5 = bf16[8,64,256]{2,1,0:T(8,128)(2,1)S(1)} async-done(((bf16[8,64,256]{2,1,0:T(8,128)(2,1)}), bf16[8,64,256]{2,1,0:T(8,128)(2,1)S(1)}, u32[]{:S(2)}, u32[]{:S(2)}) %all-to-all-start.5) | async-done | bytes 262176 | tf_op jit(solution)/shard_map/all_to_all | solution.py:488
  167.5 1.3 combine.5
  (24 shorter events, 0.1 us)
Async XLA Ops:
  4.0 60.1 %copy-start.11 = (bf16[1024,1]{0,1:T(2,128)(2,1)S(1)}, bf16[1024,1]{0,1:T(2,128)(2,1)}, u32[]{:S(2)}) copy-start(bf16[1024,1]{0,1:T(2,128)(2,1)} %param.12) | copy-start | bytes 6148
  27.8 1.0 copy-start
  28.9 0.7 copy-start.1
  29.6 0.7 copy-start.2
  30.3 0.7 copy-start.4
  47.2 17.6 %copy-start.8 = (bf16[8,80,256]{2,1,0:T(8,128)(2,1)}, bf16[8,80,256]{2,1,0:T(8,128)(2,1)S(1)}, u32[]{:S(2)}) copy-start(bf16[8,80,256]{2,1,0:T(8,128)(2,1)S(1)} %all_to_all.31) | copy-start | bytes 983044
  47.2 10.6 %collective-permute-start.5 = (bf16[640,256]{1,0:T(8,128)(2,1)S(1)}, bf16[640,256]{1,0:T(8,128)(2,1)S(1)}, u32[]{:S(2)}, u32[]{:S(2)}) collective-permute-start(bf16[640,256]{1,0:T(8,128)(2,1)S(1)} %bitcast.54), channel_id=1, source_target_pairs={{0,2},{1,3},{2,0},{3,1},{4,6},{5,7},{6,4},{7,5},{8,10},{9,11},{10,... | collective-permute-start | bytes 983048 | tf_op jit(solution)/shard_map/ppermute | solution.py:515
  48.7 26.3 %copy-start.6 = (bf16[8,112,256]{2,1,0:T(8,128)(2,1)}, bf16[8,112,256]{2,1,0:T(8,128)(2,1)S(1)}, u32[]{:S(2)}) copy-start(bf16[8,112,256]{2,1,0:T(8,128)(2,1)S(1)} %slice.28) | copy-start | bytes 1376260
  48.7 15.4 %collective-permute-start = (bf16[896,256]{1,0:T(8,128)(2,1)S(1)}, bf16[896,256]{1,0:T(8,128)(2,1)S(1)}, u32[]{:S(2)}, u32[]{:S(2)}) collective-permute-start(bf16[896,256]{1,0:T(8,128)(2,1)S(1)} %bitcast.51), channel_id=1, source_target_pairs={{0,2},{1,3},{2,0},{3,1},{4,6},{5,7},{6,4},{7,5},{8,10},{9,11},{10,... | collective-permute-start | bytes 1376264 | tf_op jit(solution)/shard_map/ppermute | solution.py:515
  49.3 15.4 %collective-permute-start.6 = (bf16[640,256]{1,0:T(8,128)(2,1)S(1)}, bf16[640,256]{1,0:T(8,128)(2,1)}, u32[]{:S(2)}, u32[]{:S(2)}) collective-permute-start(bf16[640,256]{1,0:T(8,128)(2,1)S(1)} %bitcast.55), channel_id=1, source_target_pairs={{0,1},{1,0},{2,3},{3,2},{4,5},{5,4},{6,7},{7,6},{8,9},{9,8},{10,11... | collective-permute-start | bytes 983048 | tf_op jit(solution)/shard_map/ppermute | solution.py:512
  57.8 7.0 %copy-start.15 = (bf16[640,256]{1,0:T(8,128)(2,1)}, bf16[640,256]{1,0:T(8,128)(2,1)S(1)}, u32[]{:S(2)}) copy-start(bf16[640,256]{1,0:T(8,128)(2,1)S(1)} %collective-permute-done.5.x1_hbm) | copy-start | bytes 983044
  57.8 7.0 %collective-permute-start.7 = (bf16[640,256]{1,0:T(8,128)(2,1)S(1)}, bf16[640,256]{1,0:T(8,128)(2,1)}, u32[]{:S(2)}, u32[]{:S(2)}) collective-permute-start(bf16[640,256]{1,0:T(8,128)(2,1)S(1)} %collective-permute-done.5.x1_hbm), channel_id=1, source_target_pairs={{0,1},{1,0},{2,3},{3,2},{4,5},{5,4},{6,7},{7,6},{8,9},{9,8},{10,11... | collective-permute-start | bytes 983048 | tf_op jit(solution)/shard_map/ppermute | solution.py:518
  57.8 17.8 %collective-permute-start.1 = (bf16[896,256]{1,0:T(8,128)(2,1)S(1)}, bf16[896,256]{1,0:T(8,128)(2,1)S(1)}, u32[]{:S(2)}, u32[]{:S(2)}) collective-permute-start(bf16[896,256]{1,0:T(8,128)(2,1)S(1)} %bitcast.52), channel_id=1, source_target_pairs={{0,1},{1,0},{2,3},{3,2},{4,5},{5,4},{6,7},{7,6},{8,9},{9,8},{10,11... | collective-permute-start | bytes 1376264 | tf_op jit(solution)/shard_map/ppermute | solution.py:512
  64.1 10.9 %copy-start.12 = (bf16[896,256]{1,0:T(8,128)(2,1)}, bf16[896,256]{1,0:T(8,128)(2,1)S(1)}, u32[]{:S(2)}) copy-start(bf16[896,256]{1,0:T(8,128)(2,1)S(1)} %collective-permute-done.x1_hbm) | copy-start | bytes 1376260
  64.1 11.5 %collective-permute-start.2 = (bf16[896,256]{1,0:T(8,128)(2,1)S(1)}, bf16[896,256]{1,0:T(8,128)(2,1)S(1)}, u32[]{:S(2)}, u32[]{:S(2)}) collective-permute-start(bf16[896,256]{1,0:T(8,128)(2,1)S(1)} %collective-permute-done.x1_hbm), channel_id=1, source_target_pairs={{0,1},{1,0},{2,3},{3,2},{4,5},{5,4},{6,7},{7,6},{8,9},{9,8},{10,11... | collective-permute-start | bytes 1376264 | tf_op jit(solution)/shard_map/ppermute | solution.py:518
  75.0 31.5 %copy-start.9 = (bf16[640,256]{1,0:T(8,128)(2,1)S(1)}, bf16[640,256]{1,0:T(8,128)(2,1)}, u32[]{:S(2)}) copy-start(bf16[640,256]{1,0:T(8,128)(2,1)} %get-tuple-element.28) | copy-start | bytes 983044
  75.0 31.5 %collective-permute-start.8 = (bf16[2,640,256]{2,1,0:T(8,128)(2,1)}, bf16[2,640,256]{2,1,0:T(8,128)(2,1)S(1)}, u32[]{:S(2)}, u32[]{:S(2)}) collective-permute-start(bf16[2,640,256]{2,1,0:T(8,128)(2,1)} %get-tuple-element.27), channel_id=1, source_target_pairs={{0,1},{1,0},{2,3},{3,2},{4,5},{5,4},{6,7},{7,6},{8,9},{9,8},{10,11... | collective-permute-start | bytes 1966088 | tf_op jit(solution)/shard_map/ppermute | solution.py:530
  75.6 0.8 copy-start.13
  76.3 0.8 copy-start.14
  90.4 28.9 %copy-start.7 = (bf16[640,256]{1,0:T(8,128)(2,1)S(1)}, bf16[640,256]{1,0:T(8,128)(2,1)}, u32[]{:S(2)}) copy-start(bf16[640,256]{1,0:T(8,128)(2,1)} %get-tuple-element.26) | copy-start | bytes 983044
  90.4 24.2 %collective-permute-start.3 = (bf16[2,896,256]{2,1,0:T(8,128)(2,1)}, bf16[2,896,256]{2,1,0:T(8,128)(2,1)S(1)}, u32[]{:S(2)}, u32[]{:S(2)}) collective-permute-start(bf16[2,896,256]{2,1,0:T(8,128)(2,1)} %get-tuple-element.23), channel_id=1, source_target_pairs={{0,1},{1,0},{2,3},{3,2},{4,5},{5,4},{6,7},{7,6},{8,9},{9,8},{10,11... | collective-permute-start | bytes 2752520 | tf_op jit(solution)/shard_map/ppermute | solution.py:530
  105.1 9.5 %collective-permute-start.10 = (bf16[512,256]{1,0:T(8,128)(2,1)}, bf16[512,256]{1,0:T(8,128)(2,1)}, u32[]{:S(2)}, u32[]{:S(2)}) collective-permute-start(bf16[512,256]{1,0:T(8,128)(2,1)} %bitcast.16.x0_hbm), channel_id=1, source_target_pairs={{0,2},{1,3},{2,0},{3,1},{4,6},{5,7},{6,4},{7,5},{8,10},{9,11},{10,... | collective-permute-start | bytes 786440 | tf_op jit(solution)/shard_map/ppermute | solution.py:515
  106.7 12.6 %collective-permute-start.9 = (bf16[640,256]{1,0:T(8,128)(2,1)S(1)}, bf16[640,256]{1,0:T(8,128)(2,1)S(1)}, u32[]{:S(2)}, u32[]{:S(2)}) collective-permute-start(bf16[640,256]{1,0:T(8,128)(2,1)S(1)} %fusion.3), channel_id=1, source_target_pairs={{0,2},{1,3},{2,0},{3,1},{4,6},{5,7},{6,4},{7,5},{8,10},{9,11},{10,... | collective-permute-start | bytes 983048 | tf_op jit(solution)/shard_map/ppermute | solution.py:532
  107.3 18.4 %collective-permute-start.11 = (bf16[512,256]{1,0:T(8,128)(2,1)}, bf16[512,256]{1,0:T(8,128)(2,1)}, u32[]{:S(2)}, u32[]{:S(2)}) collective-permute-start(bf16[512,256]{1,0:T(8,128)(2,1)} %bitcast.16.x0_hbm), channel_id=1, source_target_pairs={{0,1},{1,0},{2,3},{3,2},{4,5},{5,4},{6,7},{7,6},{8,9},{9,8},{10,11... | collective-permute-start | bytes 786440 | tf_op jit(solution)/shard_map/ppermute | solution.py:512
  114.6 11.1 %collective-permute-start.12 = (bf16[512,256]{1,0:T(8,128)(2,1)}, bf16[512,256]{1,0:T(8,128)(2,1)}, u32[]{:S(2)}, u32[]{:S(2)}) collective-permute-start(bf16[512,256]{1,0:T(8,128)(2,1)} %collective-permute-done.10.x1_hbm), channel_id=1, source_target_pairs={{0,1},{1,0},{2,3},{3,2},{4,5},{5,4},{6,7},{7,6},{8,9},{9,8},{10,11... | collective-permute-start | bytes 786440 | tf_op jit(solution)/shard_map/ppermute | solution.py:518
  116.5 17.4 %collective-permute-start.4 = (bf16[896,256]{1,0:T(8,128)(2,1)}, bf16[896,256]{1,0:T(8,128)(2,1)S(1)}, u32[]{:S(2)}, u32[]{:S(2)}) collective-permute-start(bf16[896,256]{1,0:T(8,128)(2,1)} %fusion), channel_id=1, source_target_pairs={{0,2},{1,3},{2,0},{3,1},{4,6},{5,7},{6,4},{7,5},{8,10},{9,11},{10,... | collective-permute-start | bytes 1376264 | tf_op jit(solution)/shard_map/ppermute | solution.py:532
  120.1 14.7 %all-to-all-start.3 = ((bf16[8,80,256]{2,1,0:T(8,128)(2,1)}), bf16[8,80,256]{2,1,0:T(8,128)(2,1)S(1)}, u32[]{:S(2)}, u32[]{:S(2)}) async-start(bf16[8,80,256]{2,1,0:T(8,128)(2,1)} %bitcast.14), calls=%async_computation.3 | async-start | bytes 655360 | tf_op jit(solution)/shard_map/all_to_all | solution.py:488
  125.7 8.2 %copy-start.5 = (bf16[896,256]{1,0:T(8,128)(2,1)S(1)}, bf16[896,256]{1,0:T(8,128)(2,1)}, u32[]{:S(2)}) copy-start(bf16[896,256]{1,0:T(8,128)(2,1)} %get-tuple-element.22) | copy-start | bytes 1376260
  133.8 7.2 %copy-start.10 = (bf16[512,256]{1,0:T(8,128)(2,1)S(1)}, bf16[512,256]{1,0:T(8,128)(2,1)}, u32[]{:S(2)}) copy-start(bf16[512,256]{1,0:T(8,128)(2,1)} %get-tuple-element.32) | copy-start | bytes 786436
  133.8 7.2 %collective-permute-start.13 = (bf16[2,512,256]{2,1,0:T(8,128)(2,1)}, bf16[2,512,256]{2,1,0:T(8,128)(2,1)S(1)}, u32[]{:S(2)}, u32[]{:S(2)}) collective-permute-start(bf16[2,512,256]{2,1,0:T(8,128)(2,1)} %get-tuple-element.31), channel_id=1, source_target_pairs={{0,1},{1,0},{2,3},{3,2},{4,5},{5,4},{6,7},{7,6},{8,9},{9,8},{10,11... | collective-permute-start | bytes 1572872 | tf_op jit(solution)/shard_map/ppermute | solution.py:530
  134.8 23.5 %copy-start.3 = (s32[3,1024]{1,0:T(4,128)S(1)}, s32[3,1024]{1,0:T(4,128)}, u32[]{:S(2)}) copy-start(s32[3,1024]{1,0:T(4,128)} %get-tuple-element.19.pos_ref) | copy-start | bytes 36868
  134.8 19.9 %all-to-all-start.1 = ((bf16[8,112,256]{2,1,0:T(8,128)(2,1)}), bf16[8,112,256]{2,1,0:T(8,128)(2,1)S(1)}, u32[]{:S(2)}, u32[]{:S(2)}) async-start(bf16[8,112,256]{2,1,0:T(8,128)(2,1)} %bitcast.8), calls=%async_computation.1 | async-start | bytes 917504 | tf_op jit(solution)/shard_map/all_to_all | solution.py:488
  141.0 8.5 %collective-permute-start.14 = (bf16[512,256]{1,0:T(8,128)(2,1)S(1)}, bf16[512,256]{1,0:T(8,128)(2,1)S(1)}, u32[]{:S(2)}, u32[]{:S(2)}) collective-permute-start(bf16[512,256]{1,0:T(8,128)(2,1)S(1)} %fusion.6), channel_id=1, source_target_pairs={{0,2},{1,3},{2,0},{3,1},{4,6},{5,7},{6,4},{7,5},{8,10},{9,11},{10,... | collective-permute-start | bytes 786440 | tf_op jit(solution)/shard_map/ppermute | solution.py:532
  154.7 12.8 %all-to-all-start.5 = ((bf16[8,64,256]{2,1,0:T(8,128)(2,1)}), bf16[8,64,256]{2,1,0:T(8,128)(2,1)S(1)}, u32[]{:S(2)}, u32[]{:S(2)}) async-start(bf16[8,64,256]{2,1,0:T(8,128)(2,1)} %bitcast.19), calls=%async_computation.5 | async-start | bytes 524288 | tf_op jit(solution)/shard_map/all_to_all | solution.py:488

commit v3 on v2

--- a/solution.py
+++ b/solution.py
@@ -316,7 +316,8 @@
     down_hbm,
     keep0_ref,
     keep1_ref,
-    give_ref,
+    give0_ref,
+    give1_ref,
     x_ref,
     normed_ref,
     hidden_ref,
@@ -400,7 +401,7 @@
     for start in starts:
         here = slice(start, start + step)
         rows = hidden_ref[here, :]
-        for target, part in zip((keep0_ref, keep1_ref, give_ref.at[0], give_ref.at[1]), order):
+        for target, part in zip((keep0_ref, keep1_ref, give0_ref, give1_ref), order):
             target[here, :] = jnp.dot(
                 rows, down_ref[:, columns(part)], preferred_element_type=f32
             ).astype(bf16)
@@ -409,16 +410,12 @@
 def expert_layer(own, pieces, places, rows, gain, router, gate_weight, up_weight, down_weight):
     width = pieces[0].shape[1]
     full, units = gate_weight.shape[1:]
-    step = next(n for n in (256, 192, 128, 64, 32, 16, 8) if rows % n == 0)
+    step = next(n for n in range(min(320, rows), 0, -8) if rows % n == 0)
     blocks = rows // step
     parts = len(pieces)
     return pl.pallas_call(
         functools.partial(expert_kernel, step=step, places=places),
-        out_shape=(
-            jax.ShapeDtypeStruct((rows, width), bf16),
-            jax.ShapeDtypeStruct((rows, width), bf16),
-            jax.ShapeDtypeStruct((2, rows, width), bf16),
-        ),
+        out_shape=(jax.ShapeDtypeStruct((rows, width), bf16),) * 4,
         in_specs=[whole_smem()]
         + [in_hbm()] * parts
         + [pl.BlockSpec(), pl.BlockSpec()]
@@ -516,7 +513,7 @@
                 mine[split * count : (split + 1) * count], "hidden", far
             )
             both = lax.ppermute(across, "hidden", near)
-            keep0, keep1, give = expert_layer(
+            keep0, keep1, give0, give1 = expert_layer(
                 own,
                 (mine, across, beside, both),
                 (split, 0, split, 0),
@@ -527,11 +524,12 @@
                 up_weight,
                 down_weight,
             )
-            got = lax.ppermute(give, "hidden", near)
-            onward = (keep1.astype(f32) + got[1].astype(f32)).astype(bf16)
+            got1 = lax.ppermute(give1, "hidden", near)
+            got0 = lax.ppermute(give0, "hidden", near)
+            onward = (keep1.astype(f32) + got1.astype(f32)).astype(bf16)
             last = lax.ppermute(onward, "hidden", far)
             whole.append(
-                (keep0.astype(f32) + got[0].astype(f32) + last.astype(f32)).astype(bf16)
+                (keep0.astype(f32) + got0.astype(f32) + last.astype(f32)).astype(bf16)
             )
         ready.append(jnp.concatenate(whole, axis=0) if len(whole) > 1 else whole[0])
     base = conv_out

time: 170 us -> 161 us (0.947)
  blocking collectives: 52 us -> 37.4 us
  starting transfers between devices: 23.8 us -> 30.5 us
  waiting for transfers between devices: 40.6 us -> 43.2 us
  Pallas kernels: 41 us -> 39.3 us
    all_to_all x3 -> x2, blocking collectives: 52 us -> 37.4 us  [exchange(): lax.all_to_all(rows, 'expert', split_axis=0, concat_axis=0, tiled=True)]
    all_to_all x3 -> x4, starting transfers between devices: 15.3 us -> 20.9 us  [exchange(): lax.all_to_all(rows, 'expert', split_axis=0, concat_axis=0, tiled=True)]
    ppermute x3, waiting for transfers between devices: 8.2 us -> 10.7 us  [shards(): last = lax.ppermute(onward, 'hidden', far)]
    pallas_call x3, Pallas kernels: 31.6 us -> 29.3 us  [expert_layer(): pl.pallas_call(functools.partial(expert_kernel, step=step, places=places)...]
    convert_element_type x6, other arithmetic: 5.58 us -> 3.87 us  [the longest x3 2.59 us: shards(): (keep0.astype(f32) + got0.astype(f32) + last.astype(f32)).astype(bf16)]
    all_to_all x3 -> x4, waiting for transfers between devices: 10.8 us -> 11.4 us  [exchange(): lax.all_to_all(rows, 'expert', split_axis=0, concat_axis=0, tiled=True)]
    unnamed x32 -> x42, local copies, waits for them, and re-layouts: 4.7 us -> 4.74 us
  transfers between devices with their start and end apart: 18 -> 22, of which waited for: 7 -> 7; matrix products, arithmetic and copies ran while one was open for 4% -> 3% of each run, Pallas kernels for 20% -> 19%
where the time goes in v3:
time: 161 us; the launch traced here: 160 us
  waiting for transfers between devices  43.2 us (27%)
  Pallas kernels  39.3 us (24%)
  blocking collectives  37.4 us (23%)
  starting transfers between devices  30.5 us (19%)
  local copies, waits for them, and re-layouts  4.99 us (3%)
  other arithmetic  4.54 us (3%)
    all_to_all x2, blocking collectives, exchange(): lax.all_to_all(rows, 'expert', split_axis=0, concat_axis=0, tiled=True)  37.4 us
    pallas_call x3, Pallas kernels, expert_layer(): pl.pallas_call(functools.partial(expert_kernel, step=step, places=places)...  29.3 us
    ppermute x3, waiting for transfers between devices, shards(): lax.ppermute(mine[split * count:(split + 1) * count], 'hidden', far)  21 us
    all_to_all x4, starting transfers between devices, exchange(): lax.all_to_all(rows, 'expert', split_axis=0, concat_axis=0, tiled=True)  20.9 us
    all_to_all x4, waiting for transfers between devices, exchange(): lax.all_to_all(rows, 'expert', split_axis=0, concat_axis=0, tiled=True)  11.4 us
    ppermute x3, waiting for transfers between devices, shards(): last = lax.ppermute(onward, 'hidden', far)  10.7 us
    unnamed x42, local copies, waits for them, and re-layouts  4.74 us
    pallas_call x1, Pallas kernels, early(): pl.pallas_call(functools.partial(early_kernel, experts=experts, capacity=...  3.97 us
  transfers between devices with their start and end apart: 22, of which 7 were waited for; matrix products, arithmetic and copies ran while one was open for 3% of the time, Pallas kernels for 19%

profile of v3, /device:TPU:0, one launch (start us, length us, event | category | flops | bytes accessed | tf_op | source)
XLA Modules:
  0.0 160.3 jit_solution(1240887436229383538)
XLA Ops:
  0.0 4.0 %early.1 = (s32[3,1024]{1,0:T(4,128)}, bf16[8,144,256]{2,1,0:T(8,128)(2,1)}) custom-call(s32[1,8]{1,0:T(1,128)} %nbr_hbm.3, s32[1,1024]{1,0:T(1,128)} %bitcast.30, bf16[1024,256]{1,0:T(8,128)(2,1)} %pix_hbm.3, f32[9,256]{1,0:T(8,128)} %weight_hbm.3), custom_call_target="tpu_custom_call" | custom-call | tf_op jit(solution)/shard_map/early/pallas_call | solution.py:201
  4.0 0.0 copy-start.13
  4.0 23.8 %all_to_all.30.rim_ref = bf16[8,144,256]{2,1,0:T(8,128)(2,1)S(1)} all-to-all(bf16[8,144,256]{2,1,0:T(8,128)(2,1)} %get-tuple-element.23), channel_id=1, replica_groups=mesh['expert'=8,'hidden'=4] {'expert'}, dimensions={0} | all-to-all | bytes 1179648 | tf_op jit(solution)/shard_map/all_to_all | solution.py:485
  27.8 1.0 copy-done
  28.9 0.7 copy-done.1
  29.6 0.7 copy-done.2
  30.3 0.7 copy-done.4
  30.9 3.3 %late.1 = (bf16[1024,256]{1,0:T(8,128)(2,1)S(1)}, bf16[8,80,256]{2,1,0:T(8,128)(2,1)S(1)}, bf16[8,64,256]{2,1,0:T(8,128)(2,1)}) custom-call(s32[1,8]{1,0:T(1,128)S(1)} %copy-done.4, s32[3,1024]{1,0:T(4,128)S(1)} %copy-done.2, bf16[1024,256]{1,0:T(8,128)(2,1)S(1)} %copy-done, f32[9,256]{1,0:T(8,128)S(1)} %copy-done.1, bf16[8,144,256]{2,1,0:T(8,128)(2,1)S(1)} %all_to_all.30.rim_ref), custom_call_target="tpu_custom_call" | custom-call | tf_op jit(solution)/shard_map/late/pallas_call | solution.py:290
  34.3 13.6 %all_to_all.31 = bf16[8,80,256]{2,1,0:T(8,128)(2,1)S(1)} all-to-all(bf16[8,80,256]{2,1,0:T(8,128)(2,1)S(1)} %get-tuple-element.29), channel_id=1, replica_groups=mesh['expert'=8,'hidden'=4] {'expert'}, dimensions={0} | all-to-all | bytes 655360 | tf_op jit(solution)/shard_map/all_to_all | solution.py:485
  47.9 1.5 collective-permute-start.6
  49.4 0.0 copy-start.6
  49.5 0.6 collective-permute-start
  50.0 0.0 collective-permute-start.7
  50.0 8.4 %collective-permute-done.6.x1_hbm = bf16[640,256]{1,0:T(8,128)(2,1)S(1)} collective-permute-done((bf16[640,256]{1,0:T(8,128)(2,1)S(1)}, bf16[640,256]{1,0:T(8,128)(2,1)S(1)}, u32[]{:S(2)}, u32[]{:S(2)}) %collective-permute-start.6) | collective-permute-done | bytes 327712 | tf_op jit(solution)/shard_map/ppermute | solution.py:512
  58.5 0.0 collective-permute-start.8
  58.5 0.5 collective-permute-start.1
  59.0 5.8 %collective-permute-done.x1_hbm = bf16[896,256]{1,0:T(8,128)(2,1)S(1)} collective-permute-done((bf16[896,256]{1,0:T(8,128)(2,1)S(1)}, bf16[896,256]{1,0:T(8,128)(2,1)S(1)}, u32[]{:S(2)}, u32[]{:S(2)}) %collective-permute-start) | collective-permute-done | bytes 458784 | tf_op jit(solution)/shard_map/ppermute | solution.py:512
  64.8 0.7 convert.1.router_ref
  65.5 5.1 %all-to-all-start.4 = ((bf16[8,64,256]{2,1,0:T(8,128)(2,1)}), bf16[8,64,256]{2,1,0:T(8,128)(2,1)S(1)}, u32[]{:S(2)}, u32[]{:S(2)}) async-start(bf16[8,64,256]{2,1,0:T(8,128)(2,1)} %get-tuple-element.34), calls=%async_computation.4 | async-start | bytes 524288 | tf_op jit(solution)/shard_map/all_to_all | solution.py:485
  70.6 0.0 collective-permute-done.7.x2_hbm
  70.6 0.0 collective-permute-done.8.x3_hbm
  70.6 0.7 copy-done.17
  71.3 0.1 copy-done.18
  71.4 9.1 %expert.4 = (bf16[640,256]{1,0:T(8,128)(2,1)}, bf16[640,256]{1,0:T(8,128)(2,1)}, bf16[640,256]{1,0:T(8,128)(2,1)}, bf16[640,256]{1,0:T(8,128)(2,1)}) custom-call(s32[1]{0:T(128)} %bitcast.2.own_ref, bf16[640,256]{1,0:T(8,128)(2,1)} %bitcast.26, bf16[640,256]{1,0:T(8,128)(2,1)} %copy-done.16, bf16[640,256]{1,0:T(8,128)(2,1)} %copy-done.17, ...), custom_call_target="tpu_custom_call" | custom-call | flops 4026531840 | bytes 8912896 | tf_op jit(solution)/shard_map/expert/pallas_call | solution.py:416
  80.6 0.2 collective-permute-start.10
  80.8 0.0 collective-permute-done.1.x2_hbm
  80.8 0.0 collective-permute-done.2.x3_hbm
  80.8 0.8 copy-done.15
  81.6 12.1 %expert.3 = (bf16[896,256]{1,0:T(8,128)(2,1)}, bf16[896,256]{1,0:T(8,128)(2,1)}, bf16[896,256]{1,0:T(8,128)(2,1)}, bf16[896,256]{1,0:T(8,128)(2,1)}) custom-call(s32[1]{0:T(128)} %bitcast.2.own_ref, bf16[896,256]{1,0:T(8,128)(2,1)} %bitcast.23, bf16[896,256]{1,0:T(8,128)(2,1)} %copy-done.14, bf16[896,256]{1,0:T(8,128)(2,1)} %copy-done.15, ...), custom_call_target="tpu_custom_call" | custom-call | flops 5637144576 | bytes 9961472 | tf_op jit(solution)/shard_map/expert/pallas_call | solution.py:416
  93.7 0.4 collective-permute-start.4
  94.1 0.0 all-to-all-done.4
  94.1 1.6 collective-permute-start.12
  95.7 0.1 add_convert_fusion.3
  95.7 0.5 collective-permute-start.11
  96.3 0.2 collective-permute-start.13
  96.5 6.8 %collective-permute-done.12.x1_hbm = bf16[512,256]{1,0:T(8,128)(2,1)S(1)} collective-permute-done((bf16[512,256]{1,0:T(8,128)(2,1)S(1)}, bf16[512,256]{1,0:T(8,128)(2,1)S(1)}, u32[]{:S(2)}, u32[]{:S(2)}) %collective-permute-start.12) | collective-permute-done | bytes 262176 | tf_op jit(solution)/shard_map/ppermute | solution.py:512
  103.3 0.0 collective-permute-start.14
  103.3 0.5 collective-permute-start.3
  103.8 1.1 add_convert_fusion.1
  104.9 0.0 collective-permute-done.9
  104.9 1.6 %collective-permute-start.5 = (bf16[896,256]{1,0:T(8,128)(2,1)S(1)}, bf16[896,256]{1,0:T(8,128)(2,1)S(1)}, u32[]{:S(2)}, u32[]{:S(2)}) collective-permute-start(bf16[896,256]{1,0:T(8,128)(2,1)S(1)} %add_convert_fusion.1), channel_id=1, source_target_pairs={{0,2},{1,3},{2,0},{3,1},{4,6},{5,7},{6,4},{7,5},{8,10},{9,11},{10,... | collective-permute-start | bytes 1376264 | tf_op jit(solution)/shard_map/ppermute | solution.py:530
  106.5 3.7 %collective-permute-done.11 = bf16[640,256]{1,0:T(8,128)(2,1)S(1)} collective-permute-done((bf16[640,256]{1,0:T(8,128)(2,1)S(1)}, bf16[640,256]{1,0:T(8,128)(2,1)S(1)}, u32[]{:S(2)}, u32[]{:S(2)}) %collective-permute-start.11) | collective-permute-done | bytes 327712 | tf_op jit(solution)/shard_map/ppermute | solution.py:530
  110.3 0.9 add_convert_fusion.2
  111.1 6.0 %all-to-all-start.3 = ((bf16[8,80,256]{2,1,0:T(8,128)(2,1)}), bf16[8,80,256]{2,1,0:T(8,128)(2,1)S(1)}, u32[]{:S(2)}, u32[]{:S(2)}) async-start(bf16[8,80,256]{2,1,0:T(8,128)(2,1)} %bitcast.10), calls=%async_computation.3 | async-start | bytes 655360 | tf_op jit(solution)/shard_map/all_to_all | solution.py:485
  117.2 0.0 collective-permute-done.13.x2_hbm
  117.2 8.1 %expert.5 = (bf16[512,256]{1,0:T(8,128)(2,1)}, bf16[512,256]{1,0:T(8,128)(2,1)}, bf16[512,256]{1,0:T(8,128)(2,1)}, bf16[512,256]{1,0:T(8,128)(2,1)}) custom-call(s32[1]{0:T(128)} %bitcast.2.own_ref, bf16[512,256]{1,0:T(8,128)(2,1)} %bitcast.29, bf16[512,256]{1,0:T(8,128)(2,1)} %copy-done.19, bf16[512,256]{1,0:T(8,128)(2,1)} %collective-permute-done.13.x2_hbm, ...), custom_call_target="tpu_custom_call" | custom-call | flops 3221225472 | bytes 8388608 | tf_op jit(solution)/shard_map/expert/pallas_call | solution.py:416
  125.3 0.1 collective-permute-start.16
  125.4 0.0 collective-permute-done.5
  125.4 0.9 add_convert_fusion
  126.3 0.0 all-to-all-done.3
  126.4 6.1 %all-to-all-start.1 = ((bf16[8,112,256]{2,1,0:T(8,128)(2,1)}), bf16[8,112,256]{2,1,0:T(8,128)(2,1)S(1)}, u32[]{:S(2)}, u32[]{:S(2)}) async-start(bf16[8,112,256]{2,1,0:T(8,128)(2,1)} %bitcast.6), calls=%async_computation.1 | async-start | bytes 917504 | tf_op jit(solution)/shard_map/all_to_all | solution.py:485
  132.5 0.3 collective-permute-start.15
  132.7 0.0 collective-permute-done.16
  132.8 0.1 add_convert_fusion.5
  132.8 1.6 collective-permute-start.17
  134.4 7.0 %collective-permute-done.17 = bf16[512,256]{1,0:T(8,128)(2,1)S(1)} collective-permute-done((bf16[512,256]{1,0:T(8,128)(2,1)S(1)}, bf16[512,256]{1,0:T(8,128)(2,1)S(1)}, u32[]{:S(2)}, u32[]{:S(2)}) %collective-permute-start.17) | collective-permute-done | bytes 262176 | tf_op jit(solution)/shard_map/ppermute | solution.py:530
  141.4 0.8 add_convert_fusion.4
  142.2 4.0 %all-to-all-done.1 = bf16[8,112,256]{2,1,0:T(8,128)(2,1)S(1)} async-done(((bf16[8,112,256]{2,1,0:T(8,128)(2,1)}), bf16[8,112,256]{2,1,0:T(8,128)(2,1)S(1)}, u32[]{:S(2)}, u32[]{:S(2)}) %all-to-all-start.1) | async-done | bytes 458784 | tf_op jit(solution)/shard_map/all_to_all | solution.py:485
  146.2 3.6 %all-to-all-start.5 = ((bf16[8,64,256]{2,1,0:T(8,128)(2,1)}), bf16[8,64,256]{2,1,0:T(8,128)(2,1)S(1)}, u32[]{:S(2)}, u32[]{:S(2)}) async-start(bf16[8,64,256]{2,1,0:T(8,128)(2,1)} %bitcast.13), calls=%async_computation.5 | async-start | bytes 524288 | tf_op jit(solution)/shard_map/all_to_all | solution.py:485
  149.8 0.2 copy.10
  150.1 0.8 combine.3.base_ref
  150.8 0.7 combine.4.base_ref
  151.6 7.4 %all-to-all-done.5 = bf16[8,64,256]{2,1,0:T(8,128)(2,1)S(1)} async-done(((bf16[8,64,256]{2,1,0:T(8,128)(2,1)}), bf16[8,64,256]{2,1,0:T(8,128)(2,1)S(1)}, u32[]{:S(2)}, u32[]{:S(2)}) %all-to-all-start.5) | async-done | bytes 262176 | tf_op jit(solution)/shard_map/all_to_all | solution.py:485
  159.0 1.3 combine.5
  (41 shorter events, 0.1 us)
Async XLA Ops:
  4.0 60.8 %copy-start.13 = (bf16[1024,1]{0,1:T(2,128)(2,1)S(1)}, bf16[1024,1]{0,1:T(2,128)(2,1)}, u32[]{:S(2)}) copy-start(bf16[1024,1]{0,1:T(2,128)(2,1)} %param.12) | copy-start | bytes 6148
  27.8 1.0 copy-start
  28.9 0.7 copy-start.1
  29.6 0.7 copy-start.2
  30.3 0.7 copy-start.4
  47.9 22.7 %copy-start.8 = (bf16[8,80,256]{2,1,0:T(8,128)(2,1)}, bf16[8,80,256]{2,1,0:T(8,128)(2,1)S(1)}, u32[]{:S(2)}) copy-start(bf16[8,80,256]{2,1,0:T(8,128)(2,1)S(1)} %all_to_all.31) | copy-start | bytes 983044
  47.9 10.6 %collective-permute-start.6 = (bf16[640,256]{1,0:T(8,128)(2,1)S(1)}, bf16[640,256]{1,0:T(8,128)(2,1)S(1)}, u32[]{:S(2)}, u32[]{:S(2)}) collective-permute-start(bf16[640,256]{1,0:T(8,128)(2,1)S(1)} %bitcast.24), channel_id=1, source_target_pairs={{0,2},{1,3},{2,0},{3,1},{4,6},{5,7},{6,4},{7,5},{8,10},{9,11},{10,... | collective-permute-start | bytes 983048 | tf_op jit(solution)/shard_map/ppermute | solution.py:512
  49.4 31.1 %copy-start.6 = (bf16[8,112,256]{2,1,0:T(8,128)(2,1)}, bf16[8,112,256]{2,1,0:T(8,128)(2,1)S(1)}, u32[]{:S(2)}) copy-start(bf16[8,112,256]{2,1,0:T(8,128)(2,1)S(1)} %slice.4) | copy-start | bytes 1376260
  49.5 15.3 %collective-permute-start = (bf16[896,256]{1,0:T(8,128)(2,1)S(1)}, bf16[896,256]{1,0:T(8,128)(2,1)S(1)}, u32[]{:S(2)}, u32[]{:S(2)}) collective-permute-start(bf16[896,256]{1,0:T(8,128)(2,1)S(1)} %bitcast.21), channel_id=1, source_target_pairs={{0,2},{1,3},{2,0},{3,1},{4,6},{5,7},{6,4},{7,5},{8,10},{9,11},{10,... | collective-permute-start | bytes 1376264 | tf_op jit(solution)/shard_map/ppermute | solution.py:512
  50.0 20.6 %collective-permute-start.7 = (bf16[640,256]{1,0:T(8,128)(2,1)S(1)}, bf16[640,256]{1,0:T(8,128)(2,1)S(1)}, u32[]{:S(2)}, u32[]{:S(2)}) collective-permute-start(bf16[640,256]{1,0:T(8,128)(2,1)S(1)} %bitcast.25), channel_id=1, source_target_pairs={{0,1},{1,0},{2,3},{3,2},{4,5},{5,4},{6,7},{7,6},{8,9},{9,8},{10,11... | collective-permute-start | bytes 983048 | tf_op jit(solution)/shard_map/ppermute | solution.py:509
  58.5 12.2 %copy-start.16 = (bf16[640,256]{1,0:T(8,128)(2,1)}, bf16[640,256]{1,0:T(8,128)(2,1)S(1)}, u32[]{:S(2)}) copy-start(bf16[640,256]{1,0:T(8,128)(2,1)S(1)} %collective-permute-done.6.x1_hbm) | copy-start | bytes 983044
  58.5 12.1 %collective-permute-start.8 = (bf16[640,256]{1,0:T(8,128)(2,1)S(1)}, bf16[640,256]{1,0:T(8,128)(2,1)S(1)}, u32[]{:S(2)}, u32[]{:S(2)}) collective-permute-start(bf16[640,256]{1,0:T(8,128)(2,1)S(1)} %collective-permute-done.6.x1_hbm), channel_id=1, source_target_pairs={{0,1},{1,0},{2,3},{3,2},{4,5},{5,4},{6,7},{7,6},{8,9},{9,8},{10,11... | collective-permute-start | bytes 983048 | tf_op jit(solution)/shard_map/ppermute | solution.py:515
  58.5 22.3 %collective-permute-start.1 = (bf16[896,256]{1,0:T(8,128)(2,1)S(1)}, bf16[896,256]{1,0:T(8,128)(2,1)S(1)}, u32[]{:S(2)}, u32[]{:S(2)}) collective-permute-start(bf16[896,256]{1,0:T(8,128)(2,1)S(1)} %bitcast.22), channel_id=1, source_target_pairs={{0,1},{1,0},{2,3},{3,2},{4,5},{5,4},{6,7},{7,6},{8,9},{9,8},{10,11... | collective-permute-start | bytes 1376264 | tf_op jit(solution)/shard_map/ppermute | solution.py:509
  64.8 15.8 %copy-start.14 = (bf16[896,256]{1,0:T(8,128)(2,1)}, bf16[896,256]{1,0:T(8,128)(2,1)S(1)}, u32[]{:S(2)}) copy-start(bf16[896,256]{1,0:T(8,128)(2,1)S(1)} %collective-permute-done.x1_hbm) | copy-start | bytes 1376260
  64.8 16.0 %collective-permute-start.2 = (bf16[896,256]{1,0:T(8,128)(2,1)S(1)}, bf16[896,256]{1,0:T(8,128)(2,1)}, u32[]{:S(2)}, u32[]{:S(2)}) collective-permute-start(bf16[896,256]{1,0:T(8,128)(2,1)S(1)} %collective-permute-done.x1_hbm), channel_id=1, source_target_pairs={{0,1},{1,0},{2,3},{3,2},{4,5},{5,4},{6,7},{7,6},{8,9},{9,8},{10,11... | collective-permute-start | bytes 1376264 | tf_op jit(solution)/shard_map/ppermute | solution.py:515
  65.5 28.6 %all-to-all-start.4 = ((bf16[8,64,256]{2,1,0:T(8,128)(2,1)}), bf16[8,64,256]{2,1,0:T(8,128)(2,1)S(1)}, u32[]{:S(2)}, u32[]{:S(2)}) async-start(bf16[8,64,256]{2,1,0:T(8,128)(2,1)} %get-tuple-element.34), calls=%async_computation.4 | async-start | bytes 524288 | tf_op jit(solution)/shard_map/all_to_all | solution.py:485
  70.6 0.7 copy-start.17
  70.6 0.8 copy-start.18
  80.6 15.1 %copy-start.9 = (bf16[640,256]{1,0:T(8,128)(2,1)S(1)}, bf16[640,256]{1,0:T(8,128)(2,1)}, u32[]{:S(2)}) copy-start(bf16[640,256]{1,0:T(8,128)(2,1)} %get-tuple-element.32) | copy-start | bytes 983044
  80.6 15.1 %collective-permute-start.10 = (bf16[640,256]{1,0:T(8,128)(2,1)}, bf16[640,256]{1,0:T(8,128)(2,1)S(1)}, u32[]{:S(2)}, u32[]{:S(2)}) collective-permute-start(bf16[640,256]{1,0:T(8,128)(2,1)} %get-tuple-element.33), channel_id=1, source_target_pairs={{0,1},{1,0},{2,3},{3,2},{4,5},{5,4},{6,7},{7,6},{8,9},{9,8},{10,11... | collective-permute-start | bytes 983048 | tf_op jit(solution)/shard_map/ppermute | solution.py:527
  80.8 0.8 copy-start.15
  93.6 16.6 %copy-start.7 = (bf16[640,256]{1,0:T(8,128)(2,1)S(1)}, bf16[640,256]{1,0:T(8,128)(2,1)}, u32[]{:S(2)}) copy-start(bf16[640,256]{1,0:T(8,128)(2,1)} %get-tuple-element.30) | copy-start | bytes 983044
  93.7 9.6 %collective-permute-start.4 = (bf16[896,256]{1,0:T(8,128)(2,1)}, bf16[896,256]{1,0:T(8,128)(2,1)S(1)}, u32[]{:S(2)}, u32[]{:S(2)}) collective-permute-start(bf16[896,256]{1,0:T(8,128)(2,1)} %get-tuple-element.28), channel_id=1, source_target_pairs={{0,1},{1,0},{2,3},{3,2},{4,5},{5,4},{6,7},{7,6},{8,9},{9,8},{10,11... | collective-permute-start | bytes 1376264 | tf_op jit(solution)/shard_map/ppermute | solution.py:527
  94.1 17.1 %copy-start.11 = (bf16[8,64,256]{2,1,0:T(8,128)(2,1)}, bf16[8,64,256]{2,1,0:T(8,128)(2,1)S(1)}, u32[]{:S(2)}) copy-start(bf16[8,64,256]{2,1,0:T(8,128)(2,1)S(1)} %all-to-all-done.4) | copy-start | bytes 786436
  94.1 9.2 %collective-permute-start.12 = (bf16[512,256]{1,0:T(8,128)(2,1)S(1)}, bf16[512,256]{1,0:T(8,128)(2,1)S(1)}, u32[]{:S(2)}, u32[]{:S(2)}) collective-permute-start(bf16[512,256]{1,0:T(8,128)(2,1)S(1)} %bitcast.27), channel_id=1, source_target_pairs={{0,2},{1,3},{2,0},{3,1},{4,6},{5,7},{6,4},{7,5},{8,10},{9,11},{10,... | collective-permute-start | bytes 786440 | tf_op jit(solution)/shard_map/ppermute | solution.py:512
  95.6 9.3 %collective-permute-start.9 = (bf16[640,256]{1,0:T(8,128)(2,1)}, bf16[640,256]{1,0:T(8,128)(2,1)S(1)}, u32[]{:S(2)}, u32[]{:S(2)}) collective-permute-start(bf16[640,256]{1,0:T(8,128)(2,1)} %get-tuple-element.31), channel_id=1, source_target_pairs={{0,1},{1,0},{2,3},{3,2},{4,5},{5,4},{6,7},{7,6},{8,9},{9,8},{10,11... | collective-permute-start | bytes 983048 | tf_op jit(solution)/shard_map/ppermute | solution.py:528
  95.7 14.5 %collective-permute-start.11 = (bf16[640,256]{1,0:T(8,128)(2,1)S(1)}, bf16[640,256]{1,0:T(8,128)(2,1)S(1)}, u32[]{:S(2)}, u32[]{:S(2)}) collective-permute-start(bf16[640,256]{1,0:T(8,128)(2,1)S(1)} %add_convert_fusion.3), channel_id=1, source_target_pairs={{0,2},{1,3},{2,0},{3,1},{4,6},{5,7},{6,4},{7,5},{8,10},{9,11},{10,... | collective-permute-start | bytes 983048 | tf_op jit(solution)/shard_map/ppermute | solution.py:530
  96.3 20.9 %collective-permute-start.13 = (bf16[512,256]{1,0:T(8,128)(2,1)S(1)}, bf16[512,256]{1,0:T(8,128)(2,1)}, u32[]{:S(2)}, u32[]{:S(2)}) collective-permute-start(bf16[512,256]{1,0:T(8,128)(2,1)S(1)} %bitcast.28), channel_id=1, source_target_pairs={{0,1},{1,0},{2,3},{3,2},{4,5},{5,4},{6,7},{7,6},{8,9},{9,8},{10,11... | collective-permute-start | bytes 786440 | tf_op jit(solution)/shard_map/ppermute | solution.py:509
  103.3 13.9 %copy-start.19 = (bf16[512,256]{1,0:T(8,128)(2,1)}, bf16[512,256]{1,0:T(8,128)(2,1)S(1)}, u32[]{:S(2)}) copy-start(bf16[512,256]{1,0:T(8,128)(2,1)S(1)} %collective-permute-done.12.x1_hbm) | copy-start | bytes 786436
  103.3 13.9 %collective-permute-start.14 = (bf16[512,256]{1,0:T(8,128)(2,1)S(1)}, bf16[512,256]{1,0:T(8,128)(2,1)}, u32[]{:S(2)}, u32[]{:S(2)}) collective-permute-start(bf16[512,256]{1,0:T(8,128)(2,1)S(1)} %collective-permute-done.12.x1_hbm), channel_id=1, source_target_pairs={{0,1},{1,0},{2,3},{3,2},{4,5},{5,4},{6,7},{7,6},{8,9},{9,8},{10,11... | collective-permute-start | bytes 786440 | tf_op jit(solution)/shard_map/ppermute | solution.py:515
  103.3 22.1 %collective-permute-start.3 = (bf16[896,256]{1,0:T(8,128)(2,1)}, bf16[896,256]{1,0:T(8,128)(2,1)S(1)}, u32[]{:S(2)}, u32[]{:S(2)}) collective-permute-start(bf16[896,256]{1,0:T(8,128)(2,1)} %get-tuple-element.26), channel_id=1, source_target_pairs={{0,1},{1,0},{2,3},{3,2},{4,5},{5,4},{6,7},{7,6},{8,9},{9,8},{10,11... | collective-permute-start | bytes 1376264 | tf_op jit(solution)/shard_map/ppermute | solution.py:528
  104.9 20.5 %collective-permute-start.5 = (bf16[896,256]{1,0:T(8,128)(2,1)S(1)}, bf16[896,256]{1,0:T(8,128)(2,1)S(1)}, u32[]{:S(2)}, u32[]{:S(2)}) collective-permute-start(bf16[896,256]{1,0:T(8,128)(2,1)S(1)} %add_convert_fusion.1), channel_id=1, source_target_pairs={{0,2},{1,3},{2,0},{3,1},{4,6},{5,7},{6,4},{7,5},{8,10},{9,11},{10,... | collective-permute-start | bytes 1376264 | tf_op jit(solution)/shard_map/ppermute | solution.py:530
  111.1 15.2 %all-to-all-start.3 = ((bf16[8,80,256]{2,1,0:T(8,128)(2,1)}), bf16[8,80,256]{2,1,0:T(8,128)(2,1)S(1)}, u32[]{:S(2)}, u32[]{:S(2)}) async-start(bf16[8,80,256]{2,1,0:T(8,128)(2,1)} %bitcast.10), calls=%async_computation.3 | async-start | bytes 655360 | tf_op jit(solution)/shard_map/all_to_all | solution.py:485
  117.1 8.3 %copy-start.5 = (bf16[896,256]{1,0:T(8,128)(2,1)S(1)}, bf16[896,256]{1,0:T(8,128)(2,1)}, u32[]{:S(2)}) copy-start(bf16[896,256]{1,0:T(8,128)(2,1)} %get-tuple-element.25) | copy-start | bytes 1376260
  125.3 7.2 %copy-start.20 = (bf16[512,256]{1,0:T(8,128)(2,1)S(1)}, bf16[512,256]{1,0:T(8,128)(2,1)}, u32[]{:S(2)}) copy-start(bf16[512,256]{1,0:T(8,128)(2,1)} %get-tuple-element.36) | copy-start | bytes 786436
  125.3 7.5 %copy-start.10 = (bf16[512,256]{1,0:T(8,128)(2,1)S(1)}, bf16[512,256]{1,0:T(8,128)(2,1)}, u32[]{:S(2)}) copy-start(bf16[512,256]{1,0:T(8,128)(2,1)} %get-tuple-element.37) | copy-start | bytes 786436
  125.3 16.1 %copy-start.12 = (bf16[512,256]{1,0:T(8,128)(2,1)S(1)}, bf16[512,256]{1,0:T(8,128)(2,1)}, u32[]{:S(2)}) copy-start(bf16[512,256]{1,0:T(8,128)(2,1)} %get-tuple-element.35) | copy-start | bytes 786436
  125.3 7.4 %collective-permute-start.16 = (bf16[512,256]{1,0:T(8,128)(2,1)}, bf16[512,256]{1,0:T(8,128)(2,1)S(1)}, u32[]{:S(2)}, u32[]{:S(2)}) collective-permute-start(bf16[512,256]{1,0:T(8,128)(2,1)} %get-tuple-element.38), channel_id=1, source_target_pairs={{0,1},{1,0},{2,3},{3,2},{4,5},{5,4},{6,7},{7,6},{8,9},{9,8},{10,11... | collective-permute-start | bytes 786440 | tf_op jit(solution)/shard_map/ppermute | solution.py:527
  126.3 23.5 %copy-start.3 = (s32[3,1024]{1,0:T(4,128)S(1)}, s32[3,1024]{1,0:T(4,128)}, u32[]{:S(2)}) copy-start(s32[3,1024]{1,0:T(4,128)} %get-tuple-element.22.pos_ref) | copy-start | bytes 36868
  126.4 19.8 %all-to-all-start.1 = ((bf16[8,112,256]{2,1,0:T(8,128)(2,1)}), bf16[8,112,256]{2,1,0:T(8,128)(2,1)S(1)}, u32[]{:S(2)}, u32[]{:S(2)}) async-start(bf16[8,112,256]{2,1,0:T(8,128)(2,1)} %bitcast.6), calls=%async_computation.1 | async-start | bytes 917504 | tf_op jit(solution)/shard_map/all_to_all | solution.py:485
  132.5 1.9 %collective-permute-start.15 = (bf16[512,256]{1,0:T(8,128)(2,1)S(1)}, bf16[512,256]{1,0:T(8,128)(2,1)S(1)}, u32[]{:S(2)}, u32[]{:S(2)}) collective-permute-start(bf16[512,256]{1,0:T(8,128)(2,1)S(1)} %copy-done.20), channel_id=1, source_target_pairs={{0,1},{1,0},{2,3},{3,2},{4,5},{5,4},{6,7},{7,6},{8,9},{9,8},{10,11... | collective-permute-start | bytes 786440 | tf_op jit(solution)/shard_map/ppermute | solution.py:528
  132.8 8.6 %collective-permute-start.17 = (bf16[512,256]{1,0:T(8,128)(2,1)S(1)}, bf16[512,256]{1,0:T(8,128)(2,1)S(1)}, u32[]{:S(2)}, u32[]{:S(2)}) collective-permute-start(bf16[512,256]{1,0:T(8,128)(2,1)S(1)} %add_convert_fusion.5), channel_id=1, source_target_pairs={{0,2},{1,3},{2,0},{3,1},{4,6},{5,7},{6,4},{7,5},{8,10},{9,11},{10,... | collective-permute-start | bytes 786440 | tf_op jit(solution)/shard_map/ppermute | solution.py:530
  146.2 12.8 %all-to-all-start.5 = ((bf16[8,64,256]{2,1,0:T(8,128)(2,1)}), bf16[8,64,256]{2,1,0:T(8,128)(2,1)S(1)}, u32[]{:S(2)}, u32[]{:S(2)}) async-start(bf16[8,64,256]{2,1,0:T(8,128)(2,1)} %bitcast.13), calls=%async_computation.5 | async-start | bytes 524288 | tf_op jit(solution)/shard_map/all_to_all | solution.py:485
